TPU v7x, 128 devices: a whole 4x4x4 slice. The times are simulated.
128 devices in a mesh: dp: 16 (over y_hi, x, core), hid: 8 (over y_lo, z).
Axes of the slice: x: 4, y: 4 (y_hi: 2, y_lo: 2; y = y_hi * 2 + y_lo), z: 4, core: 2. Of those that a mesh axis runs over, the one named last changes fastest.
Arguments:
- train_x: bfloat16 [4096, 4096], P('dp', 'hid'), may hold values from -6 to 6
- gate_pre: bfloat16 [4096, 14336], P('dp', 'hid'), may hold values from -6 to 6
- up_pre: bfloat16 [4096, 14336], P('dp', 'hid'), may hold values from -6 to 6
- train_dy: bfloat16 [4096, 4096], P('dp'), may hold values from -6 to 6
- val_x: bfloat16 [512, 4096], P('dp', 'hid'), may hold values from -6 to 6
- val_gate: bfloat16 [512, 14336], P('dp', 'hid'), may hold values from -6 to 6
- val_up: bfloat16 [512, 14336], P('dp', 'hid'), may hold values from -6 to 6
- val_dy: bfloat16 [512, 4096], P('dp'), may hold values from -6 to 6
- down_weight: bfloat16 [14336, 4096], P('hid', 'dp'), may hold values from -0.046875 to 0.046875
Outputs:
- gate_grad: bfloat16 [4096, 14336], P('dp', 'hid')
- up_grad: bfloat16 [4096, 14336], P('dp', 'hid')
- scores: float32 [16, 2], P('dp')
All inputs are finite; a program needn't handle non-finite values.
Results may differ from a plain program's by a relative error of at most 0.0059.
Values may be sent and summed in bfloat16 or wider, within the bound.
A program may use at most 128 MiB of HBM per device.

v0:
```python
import jax
import jax.numpy as jnp
from jax import lax
from jax.sharding import PartitionSpec as P

LEN = 256


step_rate = 0.1


def side_by_side(arrays, axis, dim, along):
    widths = [a.shape[along] for a in arrays]
    both = jnp.concatenate(arrays, axis=along)
    filled = lax.all_gather(both, axis, axis=dim, tiled=True)
    return tuple(jnp.split(filled, [sum(widths[:k]) for k in range(1, len(widths))], axis=along))


def cut_along(shard, dim, peers):
    before, after = (shard.shape[:dim], shard.shape[dim + 1 :])
    return jnp.moveaxis(shard.reshape(*before, peers, -1, *after), dim, 0)


def sum_at_owner(shard, axis, dim):
    parts = cut_along(shard, dim, lax.axis_size(axis))
    arrived = lax.all_to_all(parts, axis, split_axis=0, concat_axis=0, tiled=True)
    return arrived.sum(axis=0)


def sent_to_all(shard, axis):
    copies = jnp.broadcast_to(shard, (lax.axis_size(axis), *shard.shape))
    return lax.all_to_all(copies, axis, split_axis=0, concat_axis=0, tiled=True)


def over_copies(shard, axis):
    return sent_to_all(shard, axis).sum(axis=0)


def backward_parts(hidden_cot, gate, up):
    a = gate.astype(jnp.float32)
    b = up.astype(jnp.float32)
    s = jax.nn.sigmoid(a)
    silu = a * s
    hidden = (silu * b).astype(jnp.bfloat16)
    gate_grad = (hidden_cot * b * s * (1.0 + a * (1.0 - s))).astype(jnp.bfloat16)
    up_grad = (hidden_cot * silu).astype(jnp.bfloat16)
    return (hidden, gate_grad, up_grad)


def pair_dot(left, right):
    return lax.dot_general(
        left, right, (((1,), (1,)), ((), ())), preferred_element_type=jnp.float32
    )


def per_device(train_x, gate_pre, up_pre, train_dy, val_x, val_gate, val_up, val_dy, down_weight):
    n_dp = lax.axis_size("dp")
    n_hid = lax.axis_size("hid")
    dp_me = lax.axis_index("dp")
    hid_me = lax.axis_index("hid")
    tok_rows = train_dy.shape[0]
    val_rows = val_dy.shape[0]
    width = train_x.shape[1]
    n_seq = tok_rows // LEN
    n_val = val_rows * n_dp // LEN
    piece = lax.all_gather(down_weight, "dp", axis=1, tiled=True)
    cot_train = pair_dot(train_dy, piece)
    cot_val = pair_dot(val_dy, piece)
    hidden, gate_grad, up_grad = backward_parts(cot_train, gate_pre, up_pre)
    val_hidden, val_gate_grad, val_up_grad = backward_parts(cot_val, val_gate, val_up)
    offset = hid_me * width
    train_feats = (
        train_x,
        jnp.concatenate([gate_grad, up_grad], axis=1),
        hidden,
        lax.dynamic_slice_in_dim(train_dy, offset, width, 1),
    )
    val_feats = (
        val_x,
        jnp.concatenate([val_gate_grad, val_up_grad], axis=1),
        val_hidden,
        lax.dynamic_slice_in_dim(val_dy, offset, width, 1),
    )
    share = tok_rows // n_hid
    row_seq = (hid_me * share + jnp.arange(share, dtype=jnp.int32)) // LEN
    seq_onehot = (row_seq[:, None] == jnp.arange(n_seq, dtype=jnp.int32)[None, :]).astype(
        jnp.float32
    )

    def grams(block):
        return jnp.stack([pair_dot(block[k], train_feats[k]) for k in range(4)])

    def absorb(state, block, source):
        return lax.dynamic_update_slice(state, grams(block), (0, source * val_rows, 0))

    state = jnp.zeros((4, n_dp * val_rows, tok_rows), jnp.float32)
    state = absorb(state, val_feats, dp_me)
    gathered = side_by_side((val_feats[0], val_feats[1], val_feats[2], val_feats[3]), "dp", 0, 1)

    def visit(step, current):
        source = (dp_me + step) % n_dp
        block = tuple(
            (lax.dynamic_slice_in_dim(whole, source * val_rows, val_rows, 0) for whole in gathered)
        )
        return absorb(current, block, source)

    state = lax.fori_loop(1, n_dp, visit, state)
    summed = sum_at_owner(state, "hid", 2)
    pair = summed[0] * summed[1] + summed[2] * summed[3]
    val_seq = jnp.arange(n_dp * val_rows, dtype=jnp.int32) // LEN
    val_onehot = (val_seq[:, None] == jnp.arange(n_val, dtype=jnp.int32)[None, :]).astype(
        jnp.float32
    )
    col_sums = jnp.dot(val_onehot.T, pair, precision=lax.Precision.HIGHEST)
    partial_scores = jnp.dot(col_sums, seq_onehot, precision=lax.Precision.HIGHEST).T
    scores = over_copies(partial_scores, "hid") * (-step_rate / (LEN * LEN))
    return (gate_grad, up_grad, scores)


def solution(mesh):
    return jax.shard_map(
        per_device,
        mesh=mesh,
        in_specs=(
            P("dp", "hid"),
            P("dp", "hid"),
            P("dp", "hid"),
            P("dp", None),
            P("dp", "hid"),
            P("dp", "hid"),
            P("dp", "hid"),
            P("dp", None),
            P("hid", "dp"),
        ),
        out_specs=(P("dp", "hid"), P("dp", "hid"), P("dp", None)),
        check_vma=False,
    )
```

profile of v0, /device:TPU:1, one launch (start us, length us, event | category | flops | bytes accessed | tf_op | source)
XLA Modules:
  0.0 357.2 jit_solution(11475155400102362533)
XLA Ops:
  8.7 116.5 %all-gather.3.cloned.1.call-done = bf16[1792,4096]{1,0:T(8,128)(2,1)} async-done(((bf16[1792,256]{1,0:T(8,128)(2,1)}), bf16[1792,4096]{1,0:T(8,128)(2,1)}) %all-gather.3.cloned.1.call-update) | async-done | bytes 14680080 | tf_op jit(solution)/shard_map/all_gather | solution.py:66
  125.2 10.3 %constant_dynamic-update-slice_fusion.2 = (bf16[32,6400]{1,0:T(8,128)(2,1)S(1)}, bf16[32,1792]{1,0:T(8,128)(2,1)}, f32[32,1792]{1,0:T(8,128)S(1)}) fusion(bf16[32,6400]{1,0:T(8,128)(2,1)S(1)} %constant_dynamic-update-slice_fusion.3, bf16[32,1792]{1,0:T(8,128)(2,1)} %param.16, bf16[32,1792]{1,0:T(8,128)(2,1)} %param.17, bf16[32,4096]{1,0:T(8,128)(2,1)} %param.18, ...), kind=kOutput, calls=%fused_computation.65 | convolution fusion | flops 470450176 | bytes 15630336 | tf_op jit(solution)/shard_map/dot_general | solution.py:51
  137.9 1.6 convolution_bitcast_fusion.4
  140.3 16.8 %multiply_convert_fusion = (bf16[256,1792]{1,0:T(8,128)(2,1)}, bf16[256,1792]{1,0:T(8,128)(2,1)}, bf16[256,1792]{1,0:T(8,128)(2,1)S(1)}) fusion(bf16[256,1792]{1,0:T(8,128)(2,1)} %param.12, bf16[256,1792]{1,0:T(8,128)(2,1)} %param.13, bf16[256,4096]{1,0:T(8,128)(2,1)S(1)} %copy-done, bf16[1792,4096]{1,0:T(8,128)(2,1)} %all-gather.3.cloned.1.call-done), kind=kOutput, calls=%fused_computation.27 | convolution fusion | flops 3765895168 | bytes 21364736 | tf_op jit(solution)/shard_map/dot_general | solution.py:51
  157.1 2.3 convolution_bitcast_fusion.6
  159.8 1.5 broadcast_in_dim.4
  162.0 1.4 pad_maximum_fusion
  163.4 37.7 %all-gather.5.cloned.1.call-done = bf16[512,6400]{1,0:T(8,128)(2,1)} async-done(((bf16[32,6400]{1,0:T(8,128)(2,1)}), bf16[512,6400]{1,0:T(8,128)(2,1)}) %all-gather.5.cloned.1.call-update) | async-done | bytes 6553616 | tf_op jit(solution)/shard_map/all_gather | solution.py:15
  201.1 2.3 fusion.57
  203.3 4.1 %split.17 = bf16[512,3584]{1,0:T(8,128)(2,1)} slice(bf16[512,6400]{1,0:T(8,128)(2,1)} %all-gather.5.cloned.1.call-done), slice={[0:512], [512:4096]} | slice | bytes 7340032 | tf_op jit(solution)/shard_map/split | solution.py:16
  207.4 2.9 split.18
  210.3 92.0 %while.15 = (s32[]{:T(128)}, f32[4,512,256]{2,1,0:T(8,128)}, s32[]{:T(128)}, bf16[512,512]{1,0:T(8,128)(2,1)}, bf16[256,512]{1,0:T(8,128)(2,1)S(1)}, /*index=5*/...) while((s32[]{:T(128)}, f32[4,512,256]{2,1,0:T(8,128)}, ...), condition=%wide.region_1.2_spmd, body=%wide.region_0.1_spmd.sunk | while | flops 104955920 | bytes 4079960 | solution.py:107
  210.3 0.9 convolution_bitcast_fusion.13
  211.3 1.3 convolution_bitcast_fusion.14
  212.5 2.3 convolution_bitcast_fusion.15
  214.8 1.0 convolution_bitcast_fusion.16
  217.4 1.3 convolution_bitcast_fusion.14
  218.7 2.3 convolution_bitcast_fusion.15
  221.0 1.0 convolution_bitcast_fusion.16
  223.6 1.3 convolution_bitcast_fusion.14
  224.8 2.3 convolution_bitcast_fusion.15
  227.1 1.0 convolution_bitcast_fusion.16
  229.7 1.3 convolution_bitcast_fusion.14
  231.0 2.3 convolution_bitcast_fusion.15
  233.3 1.0 convolution_bitcast_fusion.16
  235.8 1.3 convolution_bitcast_fusion.14
  237.1 2.3 convolution_bitcast_fusion.15
  239.4 1.0 convolution_bitcast_fusion.16
  241.9 1.3 convolution_bitcast_fusion.14
  243.2 2.3 convolution_bitcast_fusion.15
  245.5 1.0 convolution_bitcast_fusion.16
  248.1 1.3 convolution_bitcast_fusion.14
  249.4 2.3 convolution_bitcast_fusion.15
  251.7 1.0 convolution_bitcast_fusion.16
  254.2 1.3 convolution_bitcast_fusion.14
  255.5 2.3 convolution_bitcast_fusion.15
  257.8 1.0 convolution_bitcast_fusion.16
  260.3 1.3 convolution_bitcast_fusion.14
  261.6 2.3 convolution_bitcast_fusion.15
  263.9 1.0 convolution_bitcast_fusion.16
  266.5 1.3 convolution_bitcast_fusion.14
  267.8 2.3 convolution_bitcast_fusion.15
  270.1 1.0 convolution_bitcast_fusion.16
  272.6 1.3 convolution_bitcast_fusion.14
  273.9 2.3 convolution_bitcast_fusion.15
  276.2 1.0 convolution_bitcast_fusion.16
  278.7 1.3 convolution_bitcast_fusion.14
  280.0 2.3 convolution_bitcast_fusion.15
  282.3 1.0 convolution_bitcast_fusion.16
  284.9 1.3 convolution_bitcast_fusion.14
  286.2 2.3 convolution_bitcast_fusion.15
  288.4 1.0 convolution_bitcast_fusion.16
  291.0 1.3 convolution_bitcast_fusion.14
  292.3 2.3 convolution_bitcast_fusion.15
  294.6 1.0 convolution_bitcast_fusion.16
  297.1 1.3 convolution_bitcast_fusion.14
  298.4 2.3 convolution_bitcast_fusion.15
  300.7 1.0 convolution_bitcast_fusion.16
  302.3 2.9 copy.19
  305.2 3.2 copy.20
  308.4 4.3 %all-to-all-start = ((f32[8,4,512,32]{2,3,1,0:T(8,128)}), f32[8,4,512,32]{2,3,1,0:T(8,128)}, u32[]{:S(2)}, u32[]{:S(2)}) async-start(f32[8,4,512,32]{2,3,1,0:T(8,128)} %copy.20), calls=%async_computation | async-start | bytes 4194304 | tf_op jit(solution)/shard_map/all_to_all | solution.py:26
  312.8 26.3 %all-to-all-done = f32[8,4,512,32]{2,3,1,0:T(8,128)} async-done(((f32[8,4,512,32]{2,3,1,0:T(8,128)}), f32[8,4,512,32]{2,3,1,0:T(8,128)}, u32[]{:S(2)}, u32[]{:S(2)}) %all-to-all-start) | async-done | bytes 2097184 | tf_op jit(solution)/shard_map/all_to_all | solution.py:26
  339.0 1.8 reduce_sum.18
  341.4 8.4 %all_to_all.10 = f32[8,1,2]{2,1,0:T(1,128)S(1)} all-to-all(f32[8,1,2]{2,1,0:T(1,128)S(1)} %broadcast_in_dim.10), channel_id=1, replica_groups=mesh['dp'=16,'hid'=8] {'hid'}, dimensions={0} | all-to-all | bytes 128 | tf_op jit(solution)/shard_map/all_to_all | solution.py:32
  (71 shorter events, 30.0 us)
Async XLA Ops:
  7.2 130.7 %copy-start = (bf16[256,4096]{1,0:T(8,128)(2,1)S(1)}, bf16[256,4096]{1,0:T(8,128)(2,1)}, u32[]{:S(2)}) copy-start(bf16[256,4096]{1,0:T(8,128)(2,1)} %param.14) | copy-start | bytes 6291460
  7.2 118.0 %all-gather.3.cloned.1.call-start = ((), (), s32[]{:S(2)}) async-start(), calls=%async_computation.2 | async-start | bytes 15597568 | tf_op jit(solution)/shard_map/all_gather | solution.py:66
  7.9 193.2 %all-gather.5.cloned.1.call-start = ((), (), s32[]{:S(2)}) async-start(), calls=%async_computation.3 | async-start | bytes 6963200 | tf_op jit(solution)/shard_map/all_gather | solution.py:15
  8.7 126.8 %copy-start.2 = (bf16[32,1792]{1,0:T(8,128)(2,1)S(1)}, bf16[32,1792]{1,0:T(8,128)(2,1)}, u32[]{:S(2)}) copy-start(bf16[32,1792]{1,0:T(8,128)(2,1)} %param.16) | copy-start | bytes 344068
  8.7 127.5 %copy-start.7 = (bf16[32,1792]{1,0:T(8,128)(2,1)S(1)}, bf16[32,1792]{1,0:T(8,128)(2,1)}, u32[]{:S(2)}) copy-start(bf16[32,1792]{1,0:T(8,128)(2,1)} %param.17) | copy-start | bytes 344068
  135.5 4.0 %copy-start.1 = (bf16[256,512]{1,0:T(8,128)(2,1)S(1)}, bf16[256,512]{1,0:T(8,128)(2,1)}, u32[]{:S(2)}) copy-start(bf16[256,512]{1,0:T(8,128)(2,1)} %param.11) | copy-start | bytes 786436
  135.5 4.0 %copy-start.9 = (bf16[32,512]{1,0:T(8,128)(2,1)S(1)}, bf16[32,512]{1,0:T(8,128)(2,1)}, u32[]{:S(2)}) copy-start(bf16[32,512]{1,0:T(8,128)(2,1)} %param.15) | copy-start | bytes 98308
  137.1 0.8 copy-start.6
  157.1 2.3 copy-start.3
  157.1 2.3 copy-start.8
  159.4 2.0 copy-start.10
  159.4 2.0 copy-start.11
  159.4 2.7 copy-start.4
  159.4 2.6 copy-start.5
  308.4 30.6 %all-to-all-start = ((f32[8,4,512,32]{2,3,1,0:T(8,128)}), f32[8,4,512,32]{2,3,1,0:T(8,128)}, u32[]{:S(2)}, u32[]{:S(2)}) async-start(f32[8,4,512,32]{2,3,1,0:T(8,128)} %copy.20), calls=%async_computation | async-start | bytes 4194304 | tf_op jit(solution)/shard_map/all_to_all | solution.py:26
Sparse Core Ops, SparseCore 0:
  10.3 114.8 all-gather.2
  138.0 63.0 all-gather.4
where the time goes:
time: 361 us; the launch traced here: 357 us
  waiting for transfers between devices  181 us (50%)
  matrix products  114 us (32%)
  local copies, waits for them, and re-layouts  19.3 us (5%)
  other arithmetic  15.4 us (4%)
  between operations  14.2 us (4%)
  blocking collectives  8.39 us (2%)
  starting transfers between devices  4.41 us (1%)
    all_gather x1, waiting for transfers between devices, per_device(): piece = lax.all_gather(down_weight, 'dp', axis=1, tiled=True)  116 us
    dot_general x66, matrix products, pair_dot(): lax.dot_general(left, right, (((1,), (1,)), ((), ())), preferred_element_...  114 us
    all_gather x1, waiting for transfers between devices, side_by_side(): filled = lax.all_gather(both, axis, axis=dim, tiled=True)  37.7 us
    all_to_all x1, waiting for transfers between devices, sum_at_owner(): lax.all_to_all(parts, axis, split_axis=0, concat_axis=0, tiled=True)  26.3 us
    dynamic_update_slice x16, other arithmetic, absorb(): lax.dynamic_update_slice(state, grams(block), (0, source * val_rows, 0))  10.8 us
    split x3, local copies, waits for them, and re-layouts, side_by_side(): jnp.split(filled, [sum(widths[:k]) for k in range(1, len(widths))], axis=...  9.24 us
    all_to_all x1, blocking collectives, sent_to_all(): return lax.all_to_all(copies, axis, split_axis=0, concat_axis=0, tiled=True)  8.39 us
  transfers between devices with their start and end apart: 3, of which 3 were waited for; matrix products, arithmetic and copies ran while one was open for 7% of the time, Pallas kernels for 0%

commit v1 on v0

v1 whole, which is shorter than its diff:
```python
import functools

import jax
import jax.numpy as jnp
from jax import lax
from jax.experimental import pallas as pl
from jax.experimental.pallas import tpu as pltpu
from jax.sharding import PartitionSpec as P

LEN = 256
step_rate = 0.1
MESH = pl.DeviceIdType.MESH
BF = jnp.bfloat16
F32 = jnp.float32

TOK = 256
VAL = 32
FFL = 1792
FC = 256
NC = FFL // FC
KH = 2048
BW = 64


def dot_t(a, b):
    return lax.dot_general(a, b, (((1,), (1,)), ((), ())), preferred_element_type=F32)


def parts(cot, gate, up):
    a = gate.astype(F32)
    b = up.astype(F32)
    s = jax.nn.sigmoid(a)
    silu = a * s
    hidden = (silu * b).astype(BF)
    gate_grad = (cot * b * s * (1.0 + a * (1.0 - s))).astype(BF)
    up_grad = (cot * silu).astype(BF)
    return hidden, gate_grad, up_grad


def kernel(
    tx_h, gate_h, up_h, dy_h, vx_h, vg_h, vu_h, vdy_h, w_h,
    gg_o, ug_o, sc_o,
    wbuf, lhs, tx, tdy, gate, up, e1, vg, vu, vc, ownp, psend, precv, gg, ug, hd,
    iop, ior, ios, ioy, iof, cacc, hacc, fin_s, fin_r,
    lsem, osem, ring_s, ring_r, y_s, y_r, p_s, p_r, z_s, z_r, f_s, f_r,
):
    i_dp = lax.axis_index("dp")
    i_hid = lax.axis_index("hid")
    yh, x, k = i_dp // 8, (i_dp // 2) % 4, i_dp % 2
    yl, z = i_hid // 4, i_hid % 4
    xm, xp, x2 = (x + 3) % 4, (x + 1) % 4, (x + 2) % 4

    def dev(yh_=yh, x_=x, k_=k, yl_=yl, z_=z):
        return ((yh_ * 4 + x_) * 2 + k_, yl_ * 4 + z_)

    right, left, sib = dev(x_=xp), dev(x_=xm), dev(k_=1 - k)
    ypart, cross, ylp = dev(yh_=1 - yh), dev(yh_=1 - yh, yl_=1 - yl), dev(yl_=1 - yl)
    zdev = [dev(z_=(z + d) % 4) for d in (1, 2, 3)]
    hids = zdev + [dev(yl_=1 - yl, z_=(z + d) % 4) for d in range(4)]

    def remote(src, dst, ss, rs, to):
        return pltpu.make_async_remote_copy(
            src_ref=src, dst_ref=dst, send_sem=ss, recv_sem=rs, device_id=to, device_id_type=MESH
        )

    me_blk = x * 2 + k
    own_rows = pl.ds(pl.multiple_of(me_blk * BW + yh * VAL, VAL), VAL)
    half_cols = pl.ds(pl.multiple_of(yh * KH, KH), KH)
    hid_cols = pl.ds(pl.multiple_of(i_hid * 512, 512), 512)
    wcol = pl.ds(pl.multiple_of(me_blk * 256, 256), 256)
    local = [
        (w_h, wbuf.at[:, wcol]),
        (vx_h, e1.at[own_rows, pl.ds(0, 512)]),
        (vdy_h.at[:, hid_cols], e1.at[own_rows, pl.ds(512, 512)]),
        (vg_h, vg.at[own_rows, :]),
        (vu_h, vu.at[own_rows, :]),
        (dy_h.at[:, half_cols], lhs.at[pl.ds(0, TOK), :]),
        (vdy_h.at[:, half_cols], lhs.at[pl.ds(TOK, VAL), :]),
        (tx_h, tx),
        (dy_h.at[:, hid_cols], tdy),
        (gate_h, gate),
        (up_h, up),
    ]
    local = [pltpu.make_async_copy(a, b, lsem.at[n]) for n, (a, b) in enumerate(local)]
    for cp in local:
        cp.start()

    barrier = pltpu.get_barrier_semaphore()
    greet = [right, left, sib, ypart, cross] + hids
    for to in greet:
        pl.semaphore_signal(barrier, inc=1, device_id=to, device_id_type=MESH)
    pl.semaphore_wait(barrier, len(greet))

    class Ring:
        def __init__(self, slot, view, half):
            self.slot, self.view, self.half = slot, view, half

        def cp(self, n, ref, to):
            return remote(ref, ref, ring_s.at[self.slot, n], ring_r.at[self.slot, n], to)

        def own(self, src=None):
            for n, to in ((0, right), (1, left), (4, sib)):
                ref = self.view(x, k)
                remote(
                    ref if src is None else src, ref,
                    ring_s.at[self.slot, n], ring_r.at[self.slot, n], to,
                ).start()

        def forward(self):
            self.cp(0, self.view(xm, k), right).wait_recv()
            self.cp(2, self.half(xm, k, 0), right).start()
            self.cp(5, self.view(xm, k), sib).start()
            self.cp(1, self.view(xp, k), left).wait_recv()
            self.cp(3, self.half(xp, k, 1), left).start()
            self.cp(6, self.view(xp, k), sib).start()

        def last(self):
            self.cp(2, self.half(x2, k, 0), right).wait_recv()
            self.cp(3, self.half(x2, k, 1), left).wait_recv()
            self.cp(7, self.view(x2, k), sib).start()

        def full(self):
            for n, xx in ((4, x), (5, xm), (6, xp), (7, x2)):
                self.cp(n, self.view(xx, 1 - k), sib).wait_recv()

        def drain(self):
            for n in (0, 1, 4, 5, 6, 7):
                self.cp(n, self.view(x, k), sib).wait_send()
            for n in (2, 3):
                self.cp(n, self.half(x, k, 0), sib).wait_send()

    def wring(s):
        def view(xx, kk):
            return wbuf.at[
                pl.ds(pl.multiple_of(s * FC, FC), FC),
                pl.ds(pl.multiple_of((xx * 2 + kk) * 256, 256), 256),
            ]

        def half(xx, kk, n):
            return wbuf.at[
                pl.ds(pl.multiple_of(s * FC + n * (FC // 2), FC // 2), FC // 2),
                pl.ds(pl.multiple_of((xx * 2 + kk) * 256, 256), 256),
            ]

        return Ring(s, view, half)

    def vring(slot, buf, first, width):
        def rows(xx, kk):
            return pl.ds(pl.multiple_of((xx * 2 + kk) * BW, BW), BW)

        def view(xx, kk):
            return buf.at[rows(xx, kk), pl.ds(first, width)]

        def half(xx, kk, n):
            return buf.at[rows(xx, kk), pl.ds(first + n * (width // 2), width // 2)]

        return Ring(slot, view, half)

    def vcring(s):
        return vring(NC + s, vc, pl.multiple_of(s * FC, FC // 2), FC)

    e1ring = vring(2 * NC, e1, 0, 1024)
    vgring = vring(2 * NC + 1, vg, 0, FFL)
    vuring = vring(2 * NC + 2, vu, 0, FFL)

    def wown(s):
        wring(s).own(w_h.at[pl.ds(pl.multiple_of(s * FC, FC), FC), :])

    other_cols = pl.ds(pl.multiple_of((1 - yh) * KH + z * 512, 512), 512)
    zcol = pl.ds(pl.multiple_of(z * 512, 512), 512)
    dy_cp = [
        remote(dy_h.at[:, other_cols], lhs.at[pl.ds(288, TOK), zcol], y_s.at[0], y_r.at[0], cross),
        remote(vdy_h.at[:, other_cols], lhs.at[pl.ds(544, VAL), zcol], y_s.at[1], y_r.at[1], cross),
    ]
    for cp in dy_cp:
        cp.start()
    e1_cp = [
        remote(vx_h, e1.at[own_rows, pl.ds(0, 512)], y_s.at[2], y_r.at[2], ypart),
        remote(vdy_h.at[:, hid_cols], e1.at[own_rows, pl.ds(512, 512)], y_s.at[3], y_r.at[3], ypart),
    ]
    for cp in e1_cp:
        cp.start()
    wown(0)
    v_cp = [
        remote(vg_h, vg.at[own_rows, :], y_s.at[4], y_r.at[4], ypart),
        remote(vu_h, vu.at[own_rows, :], y_s.at[5], y_r.at[5], ypart),
    ]
    for cp in v_cp:
        cp.start()
    wown(1)
    for cp in local:
        cp.wait()
    cacc[...] = jnp.zeros_like(cacc)
    hacc[...] = jnp.zeros_like(hacc)
    for cp in e1_cp:
        cp.wait_recv()
    e1ring.own()
    wown(2)

    def z_dy(d, zz):
        ref = lhs.at[pl.ds(288, 288), pl.ds(pl.multiple_of(zz * 512, 512), 512)]
        return remote(ref, ref, z_s.at[d - 1], z_r.at[d - 1], zdev[d - 1])

    def z_rs(d):
        to = (z + d) % 4
        return remote(
            iop.at[pl.ds(to * 2, 2)], ior.at[d - 1], z_s.at[2 + d], z_r.at[2 + d], zdev[d - 1]
        )

    def z_ag(d, zz):
        ref = iof.at[pl.ds(zz * 2, 2)]
        return remote(ref, ref, z_s.at[5 + d], z_r.at[5 + d], zdev[d - 1])

    def yl_rs():
        return remote(ios.at[1 - yl], ioy, z_s.at[9], z_r.at[9], ylp)

    def yl_ag(who):
        ref = iof.at[z * 2 + who]
        return remote(ref, ref, z_s.at[10], z_r.at[10], ylp)

    def part_cp(s):
        return remote(psend.at[s], precv.at[s], p_s.at[s], p_r.at[s], ypart)

    def cols(s):
        return pl.ds(pl.multiple_of(s * FC, FC), FC)

    def out_cp(s):
        return [
            pltpu.make_async_copy(gg.at[:, cols(s)], gg_o.at[:, cols(s)], osem.at[0, s]),
            pltpu.make_async_copy(ug.at[:, cols(s)], ug_o.at[:, cols(s)], osem.at[1, s]),
        ]

    def partial_stage(s, carry):
        wring(s).full()
        res = dot_t(lhs[...], wbuf[cols(s), :])
        psend[s, 0:288, :] = res[288:576].astype(BF)
        psend[s, 288:320, :] = res[256:288].astype(BF)
        ownp[s, 0:288, :] = res[0:288]
        ownp[s, 288:320, :] = res[544:576]
        part_cp(s).start()
        return carry

    def grad_stage(s):
        part_cp(s).wait_recv()
        vcot = ownp[s, 256:320, :] + precv[s, 256:320, :].astype(F32)
        base = me_blk * BW
        vc[pl.ds(pl.multiple_of(base + yh * VAL, VAL), VAL), cols(s)] = vcot[0:32].astype(BF)
        vc[pl.ds(pl.multiple_of(base + (1 - yh) * VAL, VAL), VAL), cols(s)] = vcot[32:64].astype(BF)
        cot = ownp[s, 0:256, :] + precv[s, 0:256, :].astype(F32)
        h, g, u = parts(cot, gate[:, cols(s)], up[:, cols(s)])
        hd[:, cols(s)] = h
        gg[:, cols(s)] = g
        ug[:, cols(s)] = u
        vcring(s).own()
        for cp in out_cp(s):
            cp.start()

    def gram_stage(s, carry):
        vcring(s).full()
        h, g, u = parts(vc[:, cols(s)].astype(F32), vg[:, cols(s)], vu[:, cols(s)])
        cacc[...] += dot_t(g, gg[:, cols(s)]) + dot_t(u, ug[:, cols(s)])
        hacc[...] += dot_t(h, hd[:, cols(s)])
        return carry

    def step(i, carry):
        @pl.when(i < NC)
        def _():
            wring(i).forward()

        @pl.when(i < NC - 3)
        def _():
            wown(i + 3)

        @pl.when(i == 0)
        def _():
            for cp in dy_cp:
                cp.wait_recv()
            for d in (1, 2, 3):
                z_dy(d, z).start()
            e1ring.forward()

        @pl.when((i >= 1) & (i < NC + 1))
        def _():
            wring(i - 1).last()

        @pl.when(i == 1)
        def _():
            e1ring.last()

        @pl.when(i == 2)
        def _():
            e1ring.full()
            gi = dot_t(e1[:, 0:512], tx[...])
            go = dot_t(e1[:, 512:1024], tdy[...])
            for p in range(8):
                iop[p, 0] = gi[p * 64 : p * 64 + 64]
                iop[p, 1] = go[p * 64 : p * 64 + 64]
            for d in (1, 2, 3):
                z_rs(d).start()

        @pl.when(i == NC - 1)
        def _():
            for cp in v_cp:
                cp.wait_recv()
            vgring.own()
            vuring.own()

        @pl.when(i == 4)
        def _():
            for d in (1, 2, 3):
                z_dy(d, (z + 4 - d) % 4).wait_recv()

        lo = jnp.clip(jnp.minimum(2 * (i - 4), i - 2), 0, NC)
        hi = jnp.clip(jnp.minimum(2 * (i - 3), i - 1), 0, NC)
        lax.fori_loop(lo, hi, partial_stage, 0)

        @pl.when((i >= 5) & (i < NC + 5))
        def _():
            grad_stage(i - 5)

        @pl.when(i == 5)
        def _():
            for d in (1, 2, 3):
                z_rs(d).wait_recv()
            ios[...] = iop[pl.ds(z * 2, 2)] + ior[0] + ior[1] + ior[2]
            yl_rs().start()

        @pl.when(i == 6)
        def _():
            yl_rs().wait_recv()
            iof[z * 2 + yl] = ios[yl] + ioy[...]
            yl_ag(yl).start()

        @pl.when(i == 7)
        def _():
            yl_ag(1 - yl).wait_recv()
            for d in (1, 2, 3):
                z_ag(d, z).start()

        @pl.when((i >= 6) & (i < NC + 6))
        def _():
            vcring(i - 6).forward()

        @pl.when((i >= 7) & (i < NC + 7))
        def _():
            vcring(i - 7).last()

        @pl.when(i == 8)
        def _():
            vgring.forward()

        @pl.when(i == 9)
        def _():
            vuring.forward()
            vgring.last()

        @pl.when(i == 10)
        def _():
            vuring.last()
            vgring.full()
            vuring.full()

        glo = jnp.where(i <= 10, 0, i - 8)
        ghi = jnp.where(i < 10, 0, i - 7)
        lax.fori_loop(glo, ghi, gram_stage, 0)
        return carry

    lax.fori_loop(0, NC + 8, step, 0)

    for d in (1, 2, 3):
        z_ag(d, (z + 4 - d) % 4).wait_recv()
    sums = []
    for v in (0, 1):
        acc = jnp.zeros((VAL, TOK), F32)
        for p in range(8):
            r = slice(p * 64 + v * VAL, p * 64 + v * VAL + VAL)
            q = slice(v * VAL, v * VAL + VAL)
            acc += iof[p, 0, q, :] * cacc[r, :] + iof[p, 1, q, :] * hacc[r, :]
        acc = acc[:, 0:128] + acc[:, 128:256]
        sums.append(acc[0:8] + acc[8:16] + acc[16:24] + acc[24:32])
    for v in (0, 1):
        fin_s[v * 8 : v * 8 + 8, :] = sums[v]
    fin = [remote(fin_s, fin_r.at[n], f_s.at[n], f_r.at[n], to) for n, to in enumerate(hids)]
    for cp in fin:
        cp.start()
    for cp in dy_cp + e1_cp + v_cp:
        cp.wait_send()
    for d in (1, 2, 3):
        z_dy(d, z).wait_send()
        z_rs(d).wait_send()
        z_ag(d, z).wait_send()
    yl_rs().wait_send()
    yl_ag(yl).wait_send()
    e1ring.drain()
    vgring.drain()
    vuring.drain()

    def drain(s, carry):
        wring(s).drain()
        vcring(s).drain()
        part_cp(s).wait_send()
        for cp in out_cp(s):
            cp.wait()
        return carry

    lax.fori_loop(0, NC, drain, 0)
    for cp in fin:
        cp.wait()
    total = fin_s[...]
    for n in range(7):
        total = total + fin_r[n]
    scale = -step_rate / (LEN * LEN)
    s0 = jnp.sum(total[0:8]) * scale
    s1 = jnp.sum(total[8:16]) * scale
    lane = lax.broadcasted_iota(jnp.int32, (1, 2), 1)
    sc_o[...] = jnp.where(lane == 0, s0, s1)


def per_device(*args):
    vm = pltpu.VMEM
    dma = pltpu.SemaphoreType.DMA
    hbm = pl.BlockSpec(memory_space=pl.ANY)
    return pl.pallas_call(
        kernel,
        out_shape=(
            jax.ShapeDtypeStruct((TOK, FFL), BF),
            jax.ShapeDtypeStruct((TOK, FFL), BF),
            jax.ShapeDtypeStruct((1, 2), F32),
        ),
        in_specs=[hbm] * 9,
        out_specs=(hbm, hbm, pl.BlockSpec(memory_space=pltpu.VMEM)),
        scratch_shapes=[
            vm((FFL, KH), BF),
            vm((576, KH), BF),
            vm((TOK, 512), BF),
            vm((TOK, 512), BF),
            vm((TOK, FFL), BF),
            vm((TOK, FFL), BF),
            vm((512, 1024), BF),
            vm((512, FFL), BF),
            vm((512, FFL), BF),
            vm((512, FFL), BF),
            vm((NC, 320, FC), F32),
            vm((NC, 320, FC), BF),
            vm((NC, 320, FC), BF),
            vm((TOK, FFL), BF),
            vm((TOK, FFL), BF),
            vm((TOK, FFL), BF),
            vm((8, 2, 64, TOK), F32),
            vm((3, 2, 2, 64, TOK), F32),
            vm((2, 2, 64, TOK), F32),
            vm((2, 64, TOK), F32),
            vm((8, 2, 64, TOK), F32),
            vm((512, TOK), F32),
            vm((512, TOK), F32),
            vm((16, 128), F32),
            vm((7, 16, 128), F32),
            dma((11,)),
            dma((2, NC)),
            dma((2 * NC + 3, 8)),
            dma((2 * NC + 3, 8)),
            dma((6,)),
            dma((6,)),
            dma((NC,)),
            dma((NC,)),
            dma((11,)),
            dma((11,)),
            dma((7,)),
            dma((7,)),
        ],
        compiler_params=pltpu.CompilerParams(
            collective_id=0, has_side_effects=True, vmem_limit_bytes=56 * 1024 * 1024
        ),
    )(*args)


def solution(mesh):
    return jax.shard_map(
        per_device,
        mesh=mesh,
        in_specs=(
            P("dp", "hid"),
            P("dp", "hid"),
            P("dp", "hid"),
            P("dp", None),
            P("dp", "hid"),
            P("dp", "hid"),
            P("dp", "hid"),
            P("dp", None),
            P("hid", "dp"),
        ),
        out_specs=(P("dp", "hid"), P("dp", "hid"), P("dp", None)),
        check_vma=False,
    )
```

time: 361 us -> 95.7 us (0.27)
  waiting for transfers between devices: 181 us -> 0 us
  matrix products: 114 us -> 0 us
  Pallas kernels: 0 us -> 91.1 us
  local copies, waits for them, and re-layouts: 19.3 us -> 3.68 us
  other arithmetic: 15.4 us -> 0 us
  between operations: 14.2 us -> 0.66 us
  blocking collectives: 8.39 us -> 0 us
  starting transfers between devices: 4.41 us -> 0 us
    all_gather x2 -> x0, waiting for transfers between devices: 154 us -> none  [the longest x1 116 us: per_device(): piece = lax.all_gather(down_weight, 'dp', axis=1, tiled=True)]
    dot_general x68 -> x0, matrix products: 114 us -> none  [the longest x66 114 us: pair_dot(): lax.dot_general(left, right, (((1,), (1,)), ((), ())), preferred_element_...]
    pallas_call x0 -> x1, Pallas kernels: none -> 91.1 us  [per_device(): pl.pallas_call(kernel, out_shape=(jax.ShapeDtypeStruct((TOK, FFL), BF), j...]
    all_to_all x1 -> x0, waiting for transfers between devices: 26.3 us -> none  [sum_at_owner(): lax.all_to_all(parts, axis, split_axis=0, concat_axis=0, tiled=True)]
    dynamic_update_slice x16 -> x0, other arithmetic: 10.8 us -> none  [absorb(): lax.dynamic_update_slice(state, grams(block), (0, source * val_rows, 0))]
    split x3 -> x0, local copies, waits for them, and re-layouts: 9.24 us -> none  [side_by_side(): jnp.split(filled, [sum(widths[:k]) for k in range(1, len(widths))], axis=...]
    all_to_all x1 -> x0, blocking collectives: 8.39 us -> none  [sent_to_all(): return lax.all_to_all(copies, axis, split_axis=0, concat_axis=0, tiled=True)]
    all_to_all x1 -> x0, starting transfers between devices: 4.34 us -> none  [sum_at_owner(): lax.all_to_all(parts, axis, split_axis=0, concat_axis=0, tiled=True)]
  transfers between devices with their start and end apart: 3 -> 0, of which waited for: 3 -> 0; matrix products, arithmetic and copies ran while one was open for 7% -> 0% of each run, Pallas kernels for 0% -> 0%
where the time goes in v1:
time: 95.7 us; the launch traced here: 95.4 us
  Pallas kernels  91.1 us (95%)
  local copies, waits for them, and re-layouts  3.68 us (4%)
    pallas_call x1, Pallas kernels, per_device(): pl.pallas_call(kernel, out_shape=(jax.ShapeDtypeStruct((TOK, FFL), BF), j...  91.1 us
    unnamed x7, local copies, waits for them, and re-layouts  3.68 us

profile of v1, /device:TPU:1, one launch (start us, length us, event | category | flops | bytes accessed | tf_op | source)
XLA Modules:
  0.0 95.4 jit_solution(15381199142386146075)
XLA Ops:
  0.6 91.1 %shard_map.112 = (bf16[256,1792]{1,0:T(8,128)(2,1)}, bf16[256,1792]{1,0:T(8,128)(2,1)}, f32[1,2]{1,0:T(1,128)}) custom-call(bf16[256,512]{1,0:T(8,128)(2,1)} %tx_h.1, bf16[256,1792]{1,0:T(8,128)(2,1)} %gate_h.1, bf16[256,1792]{1,0:T(8,128)(2,1)} %up_h.1, bf16[256,4096]{1,0:T(8,128)(2,1)} %dy_h.1, bf16[32,512]{1,0:T(8,128)(2,1)} %vx_h.1, ...), custom_call_target="tpu_custom_call" | custom-call | tf_op jit(solution)/shard_map/pallas_call | solution.py:423
  91.7 0.0 copy-start
  91.7 0.0 copy-start.1
  91.7 2.2 %copy.15 = bf16[256,1792]{1,0:T(8,128)(2,1)} copy(bf16[256,1792]{1,0:T(8,128)(2,1)} %get-tuple-element.6) | data formatting | bytes 1835008
  94.0 0.0 copy-done
  94.0 0.9 copy.16
  94.9 0.0 copy-done.1
  94.9 0.5 copy.17
Async XLA Ops:
  91.7 2.3 %copy-start = (bf16[256,1792]{1,0:T(8,128)(2,1)S(1)}, bf16[256,1792]{1,0:T(8,128)(2,1)}, u32[]{:S(2)}) copy-start(bf16[256,1792]{1,0:T(8,128)(2,1)} %get-tuple-element.7) | copy-start | bytes 2752516
  91.7 3.2 %copy-start.1 = (f32[1,2]{1,0:T(1,128)S(1)}, f32[1,2]{1,0:T(1,128)}, u32[]{:S(2)}) copy-start(f32[1,2]{1,0:T(1,128)} %get-tuple-element.8) | copy-start | bytes 28

commit v2 on v1

--- a/solution.py
+++ b/solution.py
@@ -10,6 +10,7 @@
 LEN = 256
 step_rate = 0.1
 MESH = pl.DeviceIdType.MESH
+scope = jax.named_scope
 BF = jnp.bfloat16
 F32 = jnp.float32
 
@@ -39,10 +40,10 @@
 
 def kernel(
     tx_h, gate_h, up_h, dy_h, vx_h, vg_h, vu_h, vdy_h, w_h,
-    gg_o, ug_o, sc_o,
-    wbuf, lhs, tx, tdy, gate, up, e1, vg, vu, vc, ownp, psend, precv, gg, ug, hd,
+    gg, ug, sc_o,
+    wbuf, lhs, tx, tdy, gate, up, e1, vg, vu, vc, ownp, psend, precv, hd,
     iop, ior, ios, ioy, iof, cacc, hacc, fin_s, fin_r,
-    lsem, osem, ring_s, ring_r, y_s, y_r, p_s, p_r, z_s, z_r, f_s, f_r,
+    lsem, ring_s, ring_r, e_s, e_r, y_s, y_r, p_s, p_r, z_s, z_r, f_s, f_r,
 ):
     i_dp = lax.axis_index("dp")
     i_hid = lax.axis_index("hid")
@@ -86,10 +87,11 @@
         cp.start()
 
     barrier = pltpu.get_barrier_semaphore()
-    greet = [right, left, sib, ypart, cross] + hids
+    greet = [right, left, dev(x_=x2), sib, ypart, cross] + hids
     for to in greet:
         pl.semaphore_signal(barrier, inc=1, device_id=to, device_id_type=MESH)
-    pl.semaphore_wait(barrier, len(greet))
+    with scope("barrier"):
+        pl.semaphore_wait(barrier, len(greet))
 
     class Ring:
         def __init__(self, slot, view, half):
@@ -159,64 +161,80 @@
     def vcring(s):
         return vring(NC + s, vc, pl.multiple_of(s * FC, FC // 2), FC)
 
-    e1ring = vring(2 * NC, e1, 0, 1024)
-    vgring = vring(2 * NC + 1, vg, 0, FFL)
-    vuring = vring(2 * NC + 2, vu, 0, FFL)
+    vgring = vring(2 * NC, vg, 0, FFL)
+    vuring = vring(2 * NC + 1, vu, 0, FFL)
 
     def wown(s):
         wring(s).own(w_h.at[pl.ds(pl.multiple_of(s * FC, FC), FC), :])
 
     other_cols = pl.ds(pl.multiple_of((1 - yh) * KH + z * 512, 512), 512)
     zcol = pl.ds(pl.multiple_of(z * 512, 512), 512)
+
+    def yh_cp(n, src, dst, to):
+        return remote(src, dst, y_s.at[n], y_r.at[n], to)
+
+    def e1_blk(xx, kk, half_, n):
+        rows = pl.multiple_of((xx * 2 + kk) * BW + half_ * VAL, VAL)
+        return e1.at[pl.ds(rows, n), :]
+
+    xdev = (right, left, dev(x_=x2))
+    xsrc = (xm, xp, x2)
+
+    def e1_x(d, n):
+        src = vx_h if n == 0 else vdy_h.at[:, hid_cols]
+        return remote(
+            src, e1.at[own_rows, pl.ds(n * 512, 512)], e_s.at[d, n], e_r.at[d, n], xdev[d]
+        )
+
+    e1_cp = [e1_x(d, n) for d in range(3) for n in range(2)]
+
+    def e1_y(n, who):
+        xx = (x, xm, xp, x2)[n]
+        ref = e1_blk(xx, k, who, VAL)
+        return remote(ref, ref, e_s.at[3 + n, 0], e_r.at[3 + n, 0], ypart)
+
+    def e1_sib(n, kk):
+        xx = (x, xm, xp, x2)[n]
+        ref = e1_blk(xx, kk, 0, BW)
+        return remote(ref, ref, e_s.at[3 + n, 1], e_r.at[3 + n, 1], sib)
+
+    lo_rows, hi_rows = pl.ds(0, 128), pl.ds(128, 128)
     dy_cp = [
-        remote(dy_h.at[:, other_cols], lhs.at[pl.ds(288, TOK), zcol], y_s.at[0], y_r.at[0], cross),
-        remote(vdy_h.at[:, other_cols], lhs.at[pl.ds(544, VAL), zcol], y_s.at[1], y_r.at[1], cross),
+        yh_cp(0, dy_h.at[lo_rows, other_cols], lhs.at[pl.ds(288, 128), zcol], cross),
+        yh_cp(1, dy_h.at[hi_rows, other_cols], lhs.at[pl.ds(416, 128), zcol], cross),
+        yh_cp(6, vdy_h.at[:, other_cols], lhs.at[pl.ds(544, VAL), zcol], cross),
     ]
-    for cp in dy_cp:
+    v_cp = [
+        yh_cp(4, vg_h, vg.at[own_rows, :], ypart),
+        yh_cp(5, vu_h, vu.at[own_rows, :], ypart),
+    ]
+    for cp in dy_cp + e1_cp:
         cp.start()
-    e1_cp = [
-        remote(vx_h, e1.at[own_rows, pl.ds(0, 512)], y_s.at[2], y_r.at[2], ypart),
-        remote(vdy_h.at[:, hid_cols], e1.at[own_rows, pl.ds(512, 512)], y_s.at[3], y_r.at[3], ypart),
-    ]
-    for cp in e1_cp:
-        cp.start()
-    wown(0)
-    v_cp = [
-        remote(vg_h, vg.at[own_rows, :], y_s.at[4], y_r.at[4], ypart),
-        remote(vu_h, vu.at[own_rows, :], y_s.at[5], y_r.at[5], ypart),
-    ]
-    for cp in v_cp:
-        cp.start()
-    wown(1)
-    for cp in local:
-        cp.wait()
-    cacc[...] = jnp.zeros_like(cacc)
-    hacc[...] = jnp.zeros_like(hacc)
-    for cp in e1_cp:
-        cp.wait_recv()
-    e1ring.own()
-    wown(2)
-
-    def z_dy(d, zz):
-        ref = lhs.at[pl.ds(288, 288), pl.ds(pl.multiple_of(zz * 512, 512), 512)]
-        return remote(ref, ref, z_s.at[d - 1], z_r.at[d - 1], zdev[d - 1])
+    for c in range(4):
+        wown(c)
+
+    def z_dy(n, d, zz):
+        ref = lhs.at[
+            pl.ds(288 + n * 128, 128 + n * 32), pl.ds(pl.multiple_of(zz * 512, 512), 512)
+        ]
+        return remote(ref, ref, z_s.at[n, d - 1], z_r.at[n, d - 1], zdev[d - 1])
 
     def z_rs(d):
         to = (z + d) % 4
         return remote(
-            iop.at[pl.ds(to * 2, 2)], ior.at[d - 1], z_s.at[2 + d], z_r.at[2 + d], zdev[d - 1]
+            iop.at[pl.ds(to * 2, 2)], ior.at[d - 1], z_s.at[2, d - 1], z_r.at[2, d - 1], zdev[d - 1]
         )
 
     def z_ag(d, zz):
         ref = iof.at[pl.ds(zz * 2, 2)]
-        return remote(ref, ref, z_s.at[5 + d], z_r.at[5 + d], zdev[d - 1])
+        return remote(ref, ref, z_s.at[3, d - 1], z_r.at[3, d - 1], zdev[d - 1])
 
     def yl_rs():
-        return remote(ios.at[1 - yl], ioy, z_s.at[9], z_r.at[9], ylp)
+        return remote(ios.at[1 - yl], ioy, z_s.at[4, 0], z_r.at[4, 0], ylp)
 
     def yl_ag(who):
         ref = iof.at[z * 2 + who]
-        return remote(ref, ref, z_s.at[10], z_r.at[10], ylp)
+        return remote(ref, ref, z_s.at[4, 1], z_r.at[4, 1], ylp)
 
     def part_cp(s):
         return remote(psend.at[s], precv.at[s], p_s.at[s], p_r.at[s], ypart)
@@ -224,14 +242,9 @@
     def cols(s):
         return pl.ds(pl.multiple_of(s * FC, FC), FC)
 
-    def out_cp(s):
-        return [
-            pltpu.make_async_copy(gg.at[:, cols(s)], gg_o.at[:, cols(s)], osem.at[0, s]),
-            pltpu.make_async_copy(ug.at[:, cols(s)], ug_o.at[:, cols(s)], osem.at[1, s]),
-        ]
-
     def partial_stage(s, carry):
-        wring(s).full()
+        with scope("wfull"):
+            wring(s).full()
         res = dot_t(lhs[...], wbuf[cols(s), :])
         psend[s, 0:288, :] = res[288:576].astype(BF)
         psend[s, 288:320, :] = res[256:288].astype(BF)
@@ -241,7 +254,8 @@
         return carry
 
     def grad_stage(s):
-        part_cp(s).wait_recv()
+        with scope("gradwait"):
+            part_cp(s).wait_recv()
         vcot = ownp[s, 256:320, :] + precv[s, 256:320, :].astype(F32)
         base = me_blk * BW
         vc[pl.ds(pl.multiple_of(base + yh * VAL, VAL), VAL), cols(s)] = vcot[0:32].astype(BF)
@@ -252,8 +266,6 @@
         gg[:, cols(s)] = g
         ug[:, cols(s)] = u
         vcring(s).own()
-        for cp in out_cp(s):
-            cp.start()
 
     def gram_stage(s, carry):
         vcring(s).full()
@@ -262,120 +274,170 @@
         hacc[...] += dot_t(h, hd[:, cols(s)])
         return carry
 
+    cacc[...] = jnp.zeros_like(cacc)
+    hacc[...] = jnp.zeros_like(hacc)
+    with scope("dyA"):
+        dy_cp[0].wait_recv()
+        for d in (1, 2, 3):
+            z_dy(0, d, z).start()
+
     def step(i, carry):
         @pl.when(i < NC)
         def _():
-            wring(i).forward()
-
-        @pl.when(i < NC - 3)
-        def _():
-            wown(i + 3)
+            with scope("wfwd"):
+                wring(i).forward()
+
+        @pl.when(i < NC - 4)
+        def _():
+            wown(i + 4)
 
         @pl.when(i == 0)
         def _():
-            for cp in dy_cp:
-                cp.wait_recv()
-            for d in (1, 2, 3):
-                z_dy(d, z).start()
-            e1ring.forward()
-
-        @pl.when((i >= 1) & (i < NC + 1))
-        def _():
-            wring(i - 1).last()
-
-        @pl.when(i == 1)
-        def _():
-            e1ring.last()
+            with scope("dyB"):
+                dy_cp[1].wait_recv()
+                dy_cp[2].wait_recv()
+                for d in (1, 2, 3):
+                    z_dy(1, d, z).start()
+            with scope("e1x"):
+                for n in (1, 2):
+                    local[n].wait()
+                for cp in e1_cp:
+                    cp.wait_recv()
+                for n in range(4):
+                    e1_y(n, yh).start()
+                for cp in v_cp:
+                    cp.start()
 
         @pl.when(i == 2)
         def _():
-            e1ring.full()
-            gi = dot_t(e1[:, 0:512], tx[...])
-            go = dot_t(e1[:, 512:1024], tdy[...])
-            for p in range(8):
-                iop[p, 0] = gi[p * 64 : p * 64 + 64]
-                iop[p, 1] = go[p * 64 : p * 64 + 64]
-            for d in (1, 2, 3):
-                z_rs(d).start()
+            with scope("e1y"):
+                for n in range(4):
+                    e1_y(n, 1 - yh).wait_recv()
+                for n in range(4):
+                    e1_sib(n, k).start()
+
+        @pl.when((i >= 3) & (i < NC + 3))
+        def _():
+            with scope("wlast"):
+                wring(i - 3).last()
+
+        @pl.when(i == 3)
+        def _():
+            with scope("e1full"):
+                for n in range(4):
+                    e1_sib(n, 1 - k).wait_recv()
+                local[7].wait()
+                local[8].wait()
+            with scope("iogram"):
+                gi = dot_t(e1[:, 0:512], tx[...])
+                go = dot_t(e1[:, 512:1024], tdy[...])
+                for p in range(8):
+                    iop[p, 0] = gi[p * 64 : p * 64 + 64]
+                    iop[p, 1] = go[p * 64 : p * 64 + 64]
+                for d in (1, 2, 3):
+                    z_rs(d).start()
 
         @pl.when(i == NC - 1)
         def _():
-            for cp in v_cp:
-                cp.wait_recv()
-            vgring.own()
-            vuring.own()
+            with scope("vown"):
+                for cp in v_cp:
+                    cp.wait_recv()
+                local[3].wait()
+                local[4].wait()
+                vgring.own()
+                vuring.own()
 
         @pl.when(i == 4)
         def _():
-            for d in (1, 2, 3):
-                z_dy(d, (z + 4 - d) % 4).wait_recv()
-
-        lo = jnp.clip(jnp.minimum(2 * (i - 4), i - 2), 0, NC)
-        hi = jnp.clip(jnp.minimum(2 * (i - 3), i - 1), 0, NC)
-        lax.fori_loop(lo, hi, partial_stage, 0)
-
-        @pl.when((i >= 5) & (i < NC + 5))
-        def _():
-            grad_stage(i - 5)
+            with scope("zdy"):
+                for n in (0, 5, 6):
+                    local[n].wait()
+                for n in (0, 1):
+                    for d in (1, 2, 3):
+                        z_dy(n, d, (z + 4 - d) % 4).wait_recv()
+
+        with scope("part"):
+            lo = jnp.where(i == 4, 0, i - 3)
+            hi = jnp.where((i >= 4) & (i < NC + 3), i - 2, lo)
+            lax.fori_loop(lo, hi, partial_stage, 0)
+
+        @pl.when(i == 10)
+        def _():
+            with scope("vgfwd"):
+                vgring.forward()
+
+        @pl.when(i == NC + 5)
+        def _():
+            with scope("vufwd"):
+                vuring.forward()
+
+        @pl.when(i == 7)
+        def _():
+            with scope("iors"):
+                for d in (1, 2, 3):
+                    z_rs(d).wait_recv()
+                ios[...] = iop[pl.ds(z * 2, 2)] + ior[0] + ior[1] + ior[2]
+                yl_rs().start()
 
         @pl.when(i == 5)
         def _():
-            for d in (1, 2, 3):
-                z_rs(d).wait_recv()
-            ios[...] = iop[pl.ds(z * 2, 2)] + ior[0] + ior[1] + ior[2]
-            yl_rs().start()
-
-        @pl.when(i == 6)
-        def _():
-            yl_rs().wait_recv()
-            iof[z * 2 + yl] = ios[yl] + ioy[...]
-            yl_ag(yl).start()
-
-        @pl.when(i == 7)
-        def _():
-            yl_ag(1 - yl).wait_recv()
-            for d in (1, 2, 3):
-                z_ag(d, z).start()
-
-        @pl.when((i >= 6) & (i < NC + 6))
-        def _():
-            vcring(i - 6).forward()
+            for n in (9, 10):
+                local[n].wait()
 
         @pl.when((i >= 7) & (i < NC + 7))
         def _():
-            vcring(i - 7).last()
-
-        @pl.when(i == 8)
-        def _():
-            vgring.forward()
-
-        @pl.when(i == 9)
-        def _():
-            vuring.forward()
-            vgring.last()
-
-        @pl.when(i == 10)
-        def _():
-            vuring.last()
-            vgring.full()
-            vuring.full()
-
-        glo = jnp.where(i <= 10, 0, i - 8)
-        ghi = jnp.where(i < 10, 0, i - 7)
-        lax.fori_loop(glo, ghi, gram_stage, 0)
+            with scope("grad"):
+                grad_stage(i - 7)
+
+        @pl.when(i == 11)
+        def _():
+            with scope("ylrs"):
+                yl_rs().wait_recv()
+                iof[z * 2 + yl] = (ios[yl] + ioy[...]).astype(BF)
+                yl_ag(yl).start()
+
+        @pl.when(i == NC + 6)
+        def _():
+            with scope("ylag"):
+                yl_ag(1 - yl).wait_recv()
+                for d in (1, 2, 3):
+                    z_ag(d, z).start()
+
         return carry
 
-    lax.fori_loop(0, NC + 8, step, 0)
-
-    for d in (1, 2, 3):
-        z_ag(d, (z + 4 - d) % 4).wait_recv()
+    lax.fori_loop(0, NC + 7, step, 0)
+    def vc_forward(m, carry):
+        vcring(m).forward()
+        return carry
+
+    def vc_last(m, carry):
+        vcring(m).last()
+        return carry
+
+    with scope("vcfwd"):
+        lax.fori_loop(0, NC, vc_forward, 0)
+    with scope("vglast"):
+        vgring.last()
+    with scope("vulast"):
+        vuring.last()
+    with scope("vclast"):
+        lax.fori_loop(0, NC, vc_last, 0)
+    with scope("vfull"):
+        vgring.full()
+        vuring.full()
+    with scope("gram"):
+        lax.fori_loop(0, NC, gram_stage, 0)
+
+    with scope("zag"):
+        for d in (1, 2, 3):
+            z_ag(d, (z + 4 - d) % 4).wait_recv()
     sums = []
     for v in (0, 1):
         acc = jnp.zeros((VAL, TOK), F32)
         for p in range(8):
             r = slice(p * 64 + v * VAL, p * 64 + v * VAL + VAL)
             q = slice(v * VAL, v * VAL + VAL)
-            acc += iof[p, 0, q, :] * cacc[r, :] + iof[p, 1, q, :] * hacc[r, :]
+            acc += iof[p, 0, q, :].astype(F32) * cacc[r, :] + iof[p, 1, q, :].astype(F32) * hacc[r, :]
         acc = acc[:, 0:128] + acc[:, 128:256]
         sums.append(acc[0:8] + acc[8:16] + acc[16:24] + acc[24:32])
     for v in (0, 1):
@@ -386,12 +448,15 @@
     for cp in dy_cp + e1_cp + v_cp:
         cp.wait_send()
     for d in (1, 2, 3):
-        z_dy(d, z).wait_send()
+        z_dy(0, d, z).wait_send()
+        z_dy(1, d, z).wait_send()
         z_rs(d).wait_send()
         z_ag(d, z).wait_send()
     yl_rs().wait_send()
     yl_ag(yl).wait_send()
-    e1ring.drain()
+    for n in range(4):
+        e1_y(n, yh).wait_send()
+        e1_sib(n, k).wait_send()
     vgring.drain()
     vuring.drain()
 
@@ -399,13 +464,12 @@
         wring(s).drain()
         vcring(s).drain()
         part_cp(s).wait_send()
-        for cp in out_cp(s):
+        return carry
+
+    lax.fori_loop(0, NC, drain, 0)
+    with scope("finwait"):
+        for cp in fin:
             cp.wait()
-        return carry
-
-    lax.fori_loop(0, NC, drain, 0)
-    for cp in fin:
-        cp.wait()
     total = fin_s[...]
     for n in range(7):
         total = total + fin_r[n]
@@ -420,15 +484,12 @@
     vm = pltpu.VMEM
     dma = pltpu.SemaphoreType.DMA
     hbm = pl.BlockSpec(memory_space=pl.ANY)
+    vmem = pl.BlockSpec(memory_space=pltpu.VMEM)
     return pl.pallas_call(
         kernel,
-        out_shape=(
-            jax.ShapeDtypeStruct((TOK, FFL), BF),
-            jax.ShapeDtypeStruct((TOK, FFL), BF),
-            jax.ShapeDtypeStruct((1, 2), F32),
-        ),
+        out_shape=(vm((TOK, FFL), BF), vm((TOK, FFL), BF), vm((1, 2), F32)),
         in_specs=[hbm] * 9,
-        out_specs=(hbm, hbm, pl.BlockSpec(memory_space=pltpu.VMEM)),
+        out_specs=(vmem, vmem, vmem),
         scratch_shapes=[
             vm((FFL, KH), BF),
             vm((576, KH), BF),
@@ -444,27 +505,26 @@
             vm((NC, 320, FC), BF),
             vm((NC, 320, FC), BF),
             vm((TOK, FFL), BF),
-            vm((TOK, FFL), BF),
-            vm((TOK, FFL), BF),
             vm((8, 2, 64, TOK), F32),
             vm((3, 2, 2, 64, TOK), F32),
             vm((2, 2, 64, TOK), F32),
             vm((2, 64, TOK), F32),
-            vm((8, 2, 64, TOK), F32),
+            vm((8, 2, 64, TOK), BF),
             vm((512, TOK), F32),
             vm((512, TOK), F32),
             vm((16, 128), F32),
             vm((7, 16, 128), F32),
             dma((11,)),
-            dma((2, NC)),
-            dma((2 * NC + 3, 8)),
-            dma((2 * NC + 3, 8)),
-            dma((6,)),
-            dma((6,)),
+            dma((2 * NC + 2, 8)),
+            dma((2 * NC + 2, 8)),
+            dma((7, 2)),
+            dma((7, 2)),
+            dma((7,)),
+            dma((7,)),
             dma((NC,)),
             dma((NC,)),
-            dma((11,)),
-            dma((11,)),
+            dma((5, 3)),
+            dma((5, 3)),
             dma((7,)),
             dma((7,)),
         ],

time: 95.7 us -> 79.7 us (0.83)
  Pallas kernels: 91.1 us -> 76.5 us
  local copies, waits for them, and re-layouts: 3.68 us -> 2.36 us
    pallas_call x1, Pallas kernels: 91.1 us -> 76.5 us  [per_device(): pl.pallas_call(kernel, out_shape=(vm((TOK, FFL), BF), vm((TOK, FFL), BF),...]
    unnamed x7 -> x3, local copies, waits for them, and re-layouts: 3.68 us -> 2.36 us
where the time goes in v2:
time: 79.7 us; the launch traced here: 79.5 us
  Pallas kernels  76.5 us (96%)
  local copies, waits for them, and re-layouts  2.36 us (3%)
    pallas_call x1, Pallas kernels, per_device(): pl.pallas_call(kernel, out_shape=(vm((TOK, FFL), BF), vm((TOK, FFL), BF),...  76.5 us
    unnamed x3, local copies, waits for them, and re-layouts  2.36 us

profile of v2, /device:TPU:1, one launch (start us, length us, event | category | flops | bytes accessed | tf_op | source)
XLA Modules:
  0.0 79.5 jit_solution(16362100088868181632)
XLA Ops:
  0.6 76.5 %shard_map.112 = (bf16[256,1792]{1,0:T(8,128)(2,1)S(1)}, bf16[256,1792]{1,0:T(8,128)(2,1)S(1)}, f32[1,2]{1,0:T(1,128)S(1)}) custom-call(bf16[256,512]{1,0:T(8,128)(2,1)} %tx_h.1, bf16[256,1792]{1,0:T(8,128)(2,1)} %gate_h.1, bf16[256,1792]{1,0:T(8,128)(2,1)} %up_h.1, bf16[256,4096]{1,0:T(8,128)(2,1)} %dy_h.1, bf16[32,512]{1,0:T(8,128)(2,1)} %vx_h.1, ...), custom_call_target="tpu_custom_call" | custom-call | tf_op jit(solution)/shard_map/pallas_call | solution.py:488
  77.1 0.9 %copy.15 = bf16[256,1792]{1,0:T(8,128)(2,1)} copy(bf16[256,1792]{1,0:T(8,128)(2,1)S(1)} %get-tuple-element.3) | data formatting | bytes 1835008
  78.0 0.5 copy.17
  78.5 0.9 %copy.16 = bf16[256,1792]{1,0:T(8,128)(2,1)} copy(bf16[256,1792]{1,0:T(8,128)(2,1)S(1)} %get-tuple-element.4) | data formatting | bytes 1835008

commit v3 on v2

v3 whole, which is shorter than its diff:
```python
import functools

import jax
import jax.numpy as jnp
from jax import lax
from jax.experimental import pallas as pl
from jax.experimental.pallas import tpu as pltpu
from jax.sharding import PartitionSpec as P

LEN = 256
step_rate = 0.1
MESH = pl.DeviceIdType.MESH
scope = jax.named_scope
BF = jnp.bfloat16
F32 = jnp.float32

TOK = 256
VAL = 32
FFL = 1792
FC = 256
NC = FFL // FC
KH = 2048
PIECES = 4
LEAD = 3
VA, VB = 8 * FC, 6 * FC
BW = 64


def dot_t(a, b):
    return lax.dot_general(a, b, (((1,), (1,)), ((), ())), preferred_element_type=F32)


def parts(cot, gate, up):
    a = gate.astype(F32)
    b = up.astype(F32)
    s = jax.nn.sigmoid(a)
    silu = a * s
    hidden = (silu * b).astype(BF)
    gate_grad = (cot * b * s * (1.0 + a * (1.0 - s))).astype(BF)
    up_grad = (cot * silu).astype(BF)
    return hidden, gate_grad, up_grad


def kernel(
    tx_h, gate_h, up_h, dy_h, vx_h, vg_h, vu_h, vdy_h, w_h,
    gg, ug, total_o,
    wbuf, lhs, tx, tdy, gate, up, e1, vv, vc, ownp, psend, precv, hd,
    iop, ior, ios, iosb, ioy, iof, cacc, hacc, fin_s, fin_r,
    lsem, ring_s, ring_r, e_s, e_r, y_s, y_r, p_s, p_r, z_s, z_r, f_s, f_r,
):
    i_dp = lax.axis_index("dp")
    i_hid = lax.axis_index("hid")
    yh, x, k = i_dp // 8, (i_dp // 2) % 4, i_dp % 2
    yl, z = i_hid // 4, i_hid % 4
    xm, xp, x2 = (x + 3) % 4, (x + 1) % 4, (x + 2) % 4

    def dev(yh_=yh, x_=x, k_=k, yl_=yl, z_=z):
        return ((yh_ * 4 + x_) * 2 + k_, yl_ * 4 + z_)

    right, left, sib = dev(x_=xp), dev(x_=xm), dev(k_=1 - k)
    ypart, cross, ylp = dev(yh_=1 - yh), dev(yh_=1 - yh, yl_=1 - yl), dev(yl_=1 - yl)
    zdev = [dev(z_=(z + d) % 4) for d in (1, 2, 3)]
    hids = zdev + [dev(yl_=1 - yl, z_=(z + d) % 4) for d in range(4)]

    def remote(src, dst, ss, rs, to):
        return pltpu.make_async_remote_copy(
            src_ref=src, dst_ref=dst, send_sem=ss, recv_sem=rs, device_id=to, device_id_type=MESH
        )

    me_blk = x * 2 + k
    own_rows = pl.ds(pl.multiple_of(me_blk * BW + yh * VAL, VAL), VAL)
    half_cols = pl.ds(pl.multiple_of(yh * KH, KH), KH)
    hid_cols = pl.ds(pl.multiple_of(i_hid * 512, 512), 512)
    wcol = pl.ds(pl.multiple_of(me_blk * 256, 256), 256)
    local = [
        (0, w_h, wbuf.at[:, wcol]),
        (1, vx_h, e1.at[own_rows, pl.ds(0, 512)]),
        (1, vdy_h.at[:, hid_cols], e1.at[own_rows, pl.ds(512, 512)]),
        (2, dy_h.at[:, half_cols], lhs.at[pl.ds(0, TOK), :]),
        (2, vdy_h.at[:, half_cols], lhs.at[pl.ds(TOK, VAL), :]),
        (3, tx_h, tx),
        (3, dy_h.at[:, hid_cols], tdy),
        (4, gate_h, gate),
        (4, up_h, up),
    ]
    for c in range(NC):
        for n, src in enumerate((vg_h, vu_h)):
            at = pl.ds((2 * c + n) * FC, FC)
            local.append((5, src.at[:, pl.ds(c * FC, FC)], vv.at[own_rows, at]))
    for n, src, dst in local:
        pltpu.make_async_copy(src, dst, lsem.at[n]).start()

    def take(ref, sem):
        pltpu.make_async_copy(ref, ref, sem).wait()

    local_bytes = (
        wbuf.at[:, pl.ds(0, 256)],
        e1.at[pl.ds(0, VAL), :],
        lhs.at[pl.ds(0, TOK + VAL), :],
        lhs.at[pl.ds(0, 128), :],
        vc,
        vv.at[pl.ds(0, VAL), :],
    )

    def local_wait(n):
        take(local_bytes[n], lsem.at[n])

    barrier = pltpu.get_barrier_semaphore()
    greet = [right, left, dev(x_=x2), sib, ypart, cross] + hids
    for to in greet:
        pl.semaphore_signal(barrier, inc=1, device_id=to, device_id_type=MESH)
    with scope("barrier"):
        pl.semaphore_wait(barrier, len(greet))

    class Ring:
        def __init__(self, kind, slot, view, half, size):
            self.kind, self.slot, self.view, self.half, self.size = kind, slot, view, half, size

        def send(self, n, ref, to, src=None):
            remote(
                ref if src is None else src, ref, ring_s.at[self.kind], ring_r.at[self.slot, n], to
            ).start()

        def own(self, src=None):
            for n, to in ((0, right), (0, left), (2, sib)):
                self.send(n, self.view(x, k), to, src)

        def forward(self):
            take(self.size(2), ring_r.at[self.slot, 0])
            self.send(1, self.half(xm, k, 0), right)
            self.send(1, self.half(xp, k, 1), left)
            self.send(2, self.view(xm, k), sib)
            self.send(2, self.view(xp, k), sib)

        def last(self):
            take(self.size(1), ring_r.at[self.slot, 1])
            self.send(2, self.view(x2, k), sib)

        def full(self):
            take(self.size(4), ring_r.at[self.slot, 2])

    def wring(s):
        def view(xx, kk):
            return wbuf.at[
                pl.ds(pl.multiple_of(s * FC, FC), FC),
                pl.ds(pl.multiple_of((xx * 2 + kk) * 256, 256), 256),
            ]

        def half(xx, kk, n):
            return wbuf.at[
                pl.ds(pl.multiple_of(s * FC + n * (FC // 2), FC // 2), FC // 2),
                pl.ds(pl.multiple_of((xx * 2 + kk) * 256, 256), 256),
            ]

        def size(n):
            return wbuf.at[pl.ds(0, n * FC), pl.ds(0, 256)]

        return Ring(0, s, view, half, size)

    def vring(kind, slot, buf, first, width):
        def rows(xx, kk):
            return pl.ds(pl.multiple_of((xx * 2 + kk) * BW, BW), BW)

        def view(xx, kk):
            return buf.at[rows(xx, kk), pl.ds(first, width)]

        def half(xx, kk, n):
            return buf.at[rows(xx, kk), pl.ds(first + n * (width // 2), width // 2)]

        def size(n):
            return buf.at[pl.ds(0, n * BW), pl.ds(0, width)]

        return Ring(kind, slot, view, half, size)

    def vcring(s):
        return vring(1, NC + s, vc, pl.multiple_of(s * FC, FC // 2), FC)

    varing = vring(2, 2 * NC, vv, 0, VA)
    vbring = vring(2, 2 * NC + 1, vv, VA, VB)

    def wown(s):
        wring(s).own(w_h.at[pl.ds(pl.multiple_of(s * FC, FC), FC), :])

    other_cols = pl.ds(pl.multiple_of((1 - yh) * KH + z * 512, 512), 512)
    zcol = pl.ds(pl.multiple_of(z * 512, 512), 512)

    def yh_cp(n, src, dst, to):
        return remote(src, dst, y_s.at[n // 2], y_r.at[n], to)

    def e1_blk(xx, kk, half_, n):
        rows = pl.multiple_of((xx * 2 + kk) * BW + half_ * VAL, VAL)
        return e1.at[pl.ds(rows, n), :]

    xdev = (right, left, dev(x_=x2))
    xsrc = (xm, xp, x2)

    def e1_x(d, n):
        src = vx_h if n == 0 else vdy_h.at[:, hid_cols]
        return remote(
            src, e1.at[own_rows, pl.ds(n * 512, 512)], e_s, e_r.at[0], xdev[d]
        )

    e1_cp = [e1_x(d, n) for d in range(3) for n in range(2)]

    def e1_y(n, who):
        xx = (x, xm, xp, x2)[n]
        ref = e1_blk(xx, k, who, VAL)
        return remote(ref, ref, e_s, e_r.at[1], ypart)

    def e1_sib(n, kk):
        xx = (x, xm, xp, x2)[n]
        ref = e1_blk(xx, kk, 0, BW)
        return remote(ref, ref, e_s, e_r.at[2], sib)

    lo_rows, hi_rows = pl.ds(0, 128), pl.ds(128, 128)
    dy_cp = [
        yh_cp(0, dy_h.at[lo_rows, other_cols], lhs.at[pl.ds(288, 128), zcol], cross),
        yh_cp(1, dy_h.at[hi_rows, other_cols], lhs.at[pl.ds(416, 128), zcol], cross),
        yh_cp(1, vdy_h.at[:, other_cols], lhs.at[pl.ds(544, VAL), zcol], cross),
    ]
    v_cp = [
        yh_cp(2, vv.at[own_rows, pl.ds(0, VA)], vv.at[own_rows, pl.ds(0, VA)], ypart),
        yh_cp(2, vv.at[own_rows, pl.ds(VA, VB)], vv.at[own_rows, pl.ds(VA, VB)], ypart),
    ]
    for cp in dy_cp + e1_cp:
        cp.start()
    for c in range(LEAD):
        wown(c)

    def z_dy(n, d, zz):
        ref = lhs.at[
            pl.ds(288 + n * 128, 128 + n * 32), pl.ds(pl.multiple_of(zz * 512, 512), 512)
        ]
        return remote(ref, ref, z_s.at[0], z_r.at[0], zdev[d - 1])

    def z_rs(d):
        to = (z + d) % 4
        return remote(
            iop.at[pl.ds(to * 2, 2)], ior.at[d - 1], z_s.at[1], z_r.at[1], zdev[d - 1]
        )

    def z_ag(d, zz):
        ref = iof.at[pl.ds(zz * 2, 2)]
        return remote(ref, ref, z_s.at[2], z_r.at[2], zdev[d - 1])

    def yl_rs():
        return remote(iosb, ioy, z_s.at[3], z_r.at[3], ylp)

    def yl_ag(who):
        ref = iof.at[z * 2 + who]
        return remote(ref, ref, z_s.at[4], z_r.at[4], ylp)

    def part_cp(s):
        return remote(psend.at[s], precv.at[s], p_s, p_r.at[s], ypart)

    def cols(s):
        return pl.ds(pl.multiple_of(s * FC, FC), FC)

    def partial_stage(s):
        with scope("wfull"):
            wring(s).full()
        res = dot_t(lhs[...], wbuf[cols(s), :])
        psend[s, 0:288, :] = res[288:576].astype(BF)
        psend[s, 288:320, :] = res[256:288].astype(BF)
        ownp[s, 0:288, :] = res[0:288]
        ownp[s, 288:320, :] = res[544:576]
        part_cp(s).start()

    def grad_stage(s):
        with scope("gradwait"):
            part_cp(s).wait_recv()
        vcot = ownp[s, 256:320, :] + precv[s, 256:320, :].astype(F32)
        base = me_blk * BW
        vc[pl.ds(pl.multiple_of(base + yh * VAL, VAL), VAL), cols(s)] = vcot[0:32].astype(BF)
        vc[pl.ds(pl.multiple_of(base + (1 - yh) * VAL, VAL), VAL), cols(s)] = vcot[32:64].astype(BF)
        cot = ownp[s, 0:256, :] + precv[s, 0:256, :].astype(F32)
        h, g, u = parts(cot, gate[:, cols(s)], up[:, cols(s)])
        hd[:, cols(s)] = h
        gg[:, cols(s)] = g
        ug[:, cols(s)] = u
        vcring(s).own()

    def gram_stage(s):
        vcring(s).full()
        g_at, u_at = pl.multiple_of(s * 2 * FC, FC), pl.multiple_of(s * 2 * FC + FC, FC)
        h, g, u = parts(
            vc[:, cols(s)].astype(F32), vv[:, pl.ds(g_at, FC)], vv[:, pl.ds(u_at, FC)]
        )
        cacc[...] += dot_t(g, gg[:, cols(s)]) + dot_t(u, ug[:, cols(s)])
        hacc[...] += dot_t(h, hd[:, cols(s)])

    cacc[...] = jnp.zeros_like(cacc)
    hacc[...] = jnp.zeros_like(hacc)
    with scope("dyA"):
        dy_cp[0].wait_recv()
        for d in (1, 2, 3):
            z_dy(0, d, z).start()

    def step(i, carry):
        @pl.when(i < NC)
        def _():
            with scope("wfwd"):
                wring(i).forward()

        @pl.when(i < NC - LEAD)
        def _():
            wown(i + LEAD)

        @pl.when(i == 0)
        def _():
            with scope("dyB"):
                take(lhs.at[pl.ds(0, 160), pl.ds(0, 512)], y_r.at[1])
                for d in (1, 2, 3):
                    z_dy(1, d, z).start()
            with scope("e1x"):
                local_wait(1)
                take(e1.at[pl.ds(0, 3 * VAL), :], e_r.at[0])
                for n in range(4):
                    e1_y(n, yh).start()
                local_wait(5)
                for cp in v_cp:
                    cp.start()

        @pl.when(i == 2)
        def _():
            with scope("e1y"):
                take(e1.at[pl.ds(0, 4 * VAL), :], e_r.at[1])
                for n in range(4):
                    e1_sib(n, k).start()

        @pl.when((i >= 3) & (i < NC + 3))
        def _():
            with scope("wlast"):
                wring(i - 3).last()

        @pl.when(i == 3)
        def _():
            with scope("e1full"):
                take(e1.at[pl.ds(0, 4 * BW), :], e_r.at[2])
                local_wait(3)
            with scope("iogram"):
                gi = dot_t(e1[:, 0:512], tx[...])
                go = dot_t(e1[:, 512:1024], tdy[...])
                for p in range(8):
                    iop[p, 0] = gi[p * 64 : p * 64 + 64]
                    iop[p, 1] = go[p * 64 : p * 64 + 64]
                for d in (1, 2, 3):
                    z_rs(d).start()

        @pl.when(i == NC - 1)
        def _():
            with scope("vown"):
                take(vv.at[pl.ds(0, VAL), :], y_r.at[2])
                varing.own()
                vbring.own()

        @pl.when(i == 3)
        def _():
            with scope("zdy"):
                local_wait(0)
                local_wait(2)
                take(lhs.at[pl.ds(0, 288), pl.ds(0, 1536)], z_r.at[0])

        with scope("part"):
            @pl.when((i >= 3) & (i < NC + 3))
            def _():
                partial_stage(i - 3)

        @pl.when(i == 10)
        def _():
            with scope("vgfwd"):
                varing.forward()

        @pl.when(i == 7)
        def _():
            with scope("iors"):
                take(ior, z_r.at[1])
                ios[...] = iop[pl.ds(z * 2, 2)] + ior[0] + ior[1] + ior[2]
                iosb[...] = ios[1 - yl].astype(BF)
                yl_rs().start()

        @pl.when(i == 5)
        def _():
            local_wait(4)

        @pl.when((i >= 7) & (i < NC + 7))
        def _():
            with scope("grad"):
                grad_stage(i - 7)

        @pl.when(i == 10)
        def _():
            with scope("vbfwd"):
                vbring.forward()

        @pl.when(i >= 10)
        def _():
            with scope("vcfwd"):
                vcring(i - 10).forward()

        @pl.when(i == 11)
        def _():
            with scope("ylrs"):
                yl_rs().wait_recv()
                iof[z * 2 + yl] = (ios[yl] + ioy[...].astype(F32)).astype(BF)
                yl_ag(yl).start()

        @pl.when(i == NC + 6)
        def _():
            with scope("ylag"):
                yl_ag(1 - yl).wait_recv()
                for d in (1, 2, 3):
                    z_ag(d, z).start()

        return carry

    lax.fori_loop(0, NC + 7, step, 0)
    with scope("tailA"):
        vcring(4).forward()
        varing.last()
        for m in range(4):
            vcring(m).last()
        varing.full()
    for m in range(NC):
        with scope("tail"):
            if m == 1:
                vcring(5).forward()
            if m == 2:
                vbring.last()
                vcring(6).forward()
            if m == 3:
                vcring(4).last()
            if m == 4:
                vbring.full()
                vcring(5).last()
            if m == 5:
                vcring(6).last()
        with scope("gram"):
            gram_stage(m)

    with scope("zag"):
        take(iof.at[pl.ds(0, 6)], z_r.at[2])
    for v in (0, 1):
        acc = jnp.zeros((VAL, TOK), F32)
        for p in range(8):
            r = slice(p * 64 + v * VAL, p * 64 + v * VAL + VAL)
            q = slice(v * VAL, v * VAL + VAL)
            acc += iof[p, 0, q, :].astype(F32) * cacc[r, :] + iof[p, 1, q, :].astype(F32) * hacc[r, :]
        acc = acc[:, 0:128] + acc[:, 128:256]
        acc = acc[0:8] + acc[8:16] + acc[16:24] + acc[24:32]
        fin_s[v * 4 : v * 4 + 4, :] = acc[0:4] + acc[4:8]
    for n, to in enumerate(hids):
        remote(fin_s, fin_r.at[n], f_s, f_r, to).start()
    take(wbuf.at[pl.ds(0, 49 * 32), :], ring_s.at[0])
    take(vc.at[pl.ds(0, 7 * BW), :], ring_s.at[1])
    take(vv.at[pl.ds(0, 7 * BW), :], ring_s.at[2])
    take(e1.at[pl.ds(0, 480), :], e_s)
    take(lhs.at[pl.ds(0, 288), pl.ds(0, 512)], y_s.at[0])
    take(vv.at[pl.ds(0, VAL), :], y_s.at[1])
    take(psend, p_s)
    take(lhs.at[pl.ds(0, 288), pl.ds(0, 1536)], z_s.at[0])
    take(ior, z_s.at[1])
    take(iof.at[pl.ds(0, 6)], z_s.at[2])
    take(iosb, z_s.at[3])
    take(ioy, z_s.at[4])
    with scope("finwait"):
        take(fin_r, f_r)
        take(fin_r, f_s)
    total = fin_s[...]
    for n in range(7):
        total = total + fin_r[n]
    total_o[...] = total


def publish(gg, ug, total, gg_o, ug_o, sc_o, sem):
    rows = TOK // PIECES
    cps = []
    for q in range(PIECES):
        at = pl.ds(q * rows, rows)
        for n, (src, dst) in enumerate(((gg, gg_o), (ug, ug_o))):
            cps.append(pltpu.make_async_copy(src.at[at, :], dst.at[at, :], sem.at[n, q]))
    for cp in cps:
        cp.start()
    scale = -step_rate / (LEN * LEN)
    s0 = jnp.sum(total[0:4, :]) * scale
    s1 = jnp.sum(total[4:8, :]) * scale
    lane = lax.broadcasted_iota(jnp.int32, (1, 2), 1)
    sc_o[...] = jnp.where(lane == 0, s0, s1)
    for cp in cps:
        cp.wait()


def per_device(*args):
    vm = pltpu.VMEM
    dma = pltpu.SemaphoreType.DMA
    hbm = pl.BlockSpec(memory_space=pl.ANY)
    vmem = pl.BlockSpec(memory_space=pltpu.VMEM)
    outs = pl.pallas_call(
        kernel,
        out_shape=(vm((TOK, FFL), BF), vm((TOK, FFL), BF), vm((8, 128), F32)),
        in_specs=[hbm] * 9,
        out_specs=(vmem, vmem, vmem),
        scratch_shapes=[
            vm((FFL, KH), BF),
            vm((576, KH), BF),
            vm((TOK, 512), BF),
            vm((TOK, 512), BF),
            vm((TOK, FFL), BF),
            vm((TOK, FFL), BF),
            vm((512, 1024), BF),
            vm((512, VA + VB), BF),
            vm((512, FFL), BF),
            vm((NC, 320, FC), F32),
            vm((NC, 320, FC), BF),
            vm((NC, 320, FC), BF),
            vm((TOK, FFL), BF),
            vm((8, 2, 64, TOK), F32),
            vm((3, 2, 2, 64, TOK), F32),
            vm((2, 2, 64, TOK), F32),
            vm((2, 64, TOK), BF),
            vm((2, 64, TOK), BF),
            vm((8, 2, 64, TOK), BF),
            vm((512, TOK), F32),
            vm((512, TOK), F32),
            vm((8, 128), F32),
            vm((7, 8, 128), F32),
            dma((6,)),
            dma((3,)),
            dma((2 * NC + 2, 3)),
            dma,
            dma((3,)),
            dma((2,)),
            dma((3,)),
            dma,
            dma((NC,)),
            dma((5,)),
            dma((5,)),
            dma,
            dma,
        ],
        compiler_params=pltpu.CompilerParams(
            collective_id=0, has_side_effects=True, vmem_limit_bytes=56 * 1024 * 1024
        ),
    )(*args)
    outs = [pltpu.with_memory_space_constraint(o, pltpu.VMEM) for o in outs]
    return pl.pallas_call(
        publish,
        out_shape=(
            jax.ShapeDtypeStruct((TOK, FFL), BF),
            jax.ShapeDtypeStruct((TOK, FFL), BF),
            jax.ShapeDtypeStruct((1, 2), F32),
        ),
        in_specs=[vmem, vmem, vmem],
        out_specs=(hbm, hbm, vmem),
        scratch_shapes=[dma((2, PIECES))],
    )(*outs)


def solution(mesh):
    return jax.shard_map(
        per_device,
        mesh=mesh,
        in_specs=(
            P("dp", "hid"),
            P("dp", "hid"),
            P("dp", "hid"),
            P("dp", None),
            P("dp", "hid"),
            P("dp", "hid"),
            P("dp", "hid"),
            P("dp", None),
            P("hid", "dp"),
        ),
        out_specs=(P("dp", "hid"), P("dp", "hid"), P("dp", None)),
        check_vma=False,
    )
```

time: 79.7 us -> 75.6 us (0.949)
  local copies, waits for them, and re-layouts: 2.36 us -> 0 us
  Pallas kernels: 76.5 us -> 74.8 us
    pallas_call x1, Pallas kernels: 76.5 us -> 73 us  [per_device(): pl.pallas_call(kernel, out_shape=(vm((TOK, FFL), BF), vm((TOK, FFL), BF),...]
    unnamed x3 -> x0, local copies, waits for them, and re-layouts: 2.36 us -> none
    pallas_call x0 -> x1, Pallas kernels: none -> 1.8 us  [per_device(): pl.pallas_call(publish, out_shape=(jax.ShapeDtypeStruct((TOK, FFL), BF),...]
where the time goes in v3:
time: 75.6 us; the launch traced here: 75.5 us
  Pallas kernels  74.8 us (99%)
    pallas_call x1, Pallas kernels, per_device(): pl.pallas_call(kernel, out_shape=(vm((TOK, FFL), BF), vm((TOK, FFL), BF),...  73 us
    pallas_call x1, Pallas kernels, per_device(): pl.pallas_call(publish, out_shape=(jax.ShapeDtypeStruct((TOK, FFL), BF),...  1.8 us

profile of v3, /device:TPU:1, one launch (start us, length us, event | category | flops | bytes accessed | tf_op | source)
XLA Modules:
  0.0 75.5 jit_solution(16389836679808517191)
XLA Ops:
  0.6 73.0 %shard_map.112 = (bf16[256,1792]{1,0:T(8,128)(2,1)S(1)}, bf16[256,1792]{1,0:T(8,128)(2,1)S(1)}, f32[8,128]{1,0:T(8,128)S(1)}) custom-call(bf16[256,512]{1,0:T(8,128)(2,1)} %tx_h.1, bf16[256,1792]{1,0:T(8,128)(2,1)} %gate_h.1, bf16[256,1792]{1,0:T(8,128)(2,1)} %up_h.1, bf16[256,4096]{1,0:T(8,128)(2,1)} %dy_h.1, bf16[32,512]{1,0:T(8,128)(2,1)} %vx_h.1, ...), custom_call_target="tpu_custom_call" | custom-call | tf_op jit(solution)/shard_map/pallas_call | solution.py:498
  73.7 1.8 %shard_map.113 = (bf16[256,1792]{1,0:T(8,128)(2,1)}, bf16[256,1792]{1,0:T(8,128)(2,1)}, f32[1,2]{1,0:T(1,128)}) custom-call(bf16[256,1792]{1,0:T(8,128)(2,1)S(1)} %get-tuple-element.6.gg, bf16[256,1792]{1,0:T(8,128)(2,1)S(1)} %get-tuple-element.7.ug, f32[8,128]{1,0:T(8,128)S(1)} %get-tuple-element.8.total), custom_call_target="tpu_custom_call" | custom-call | tf_op jit(solution)/shard_map/pallas_call | solution.py:546

commit v4 on v3

--- a/solution.py
+++ b/solution.py
@@ -45,7 +45,7 @@
     tx_h, gate_h, up_h, dy_h, vx_h, vg_h, vu_h, vdy_h, w_h,
     gg, ug, total_o,
     wbuf, lhs, tx, tdy, gate, up, e1, vv, vc, ownp, psend, precv, hd,
-    iop, ior, ios, iosb, ioy, iof, cacc, hacc, fin_s, fin_r,
+    iop, ior, ios, iosb, ioy, iof, iofb, iofo, cacc, hacc, fin_s, fin_r,
     lsem, ring_s, ring_r, e_s, e_r, y_s, y_r, p_s, p_r, z_s, z_r, f_s, f_r,
 ):
     i_dp = lax.axis_index("dp")
@@ -185,7 +185,7 @@
     zcol = pl.ds(pl.multiple_of(z * 512, 512), 512)
 
     def yh_cp(n, src, dst, to):
-        return remote(src, dst, y_s.at[n // 2], y_r.at[n], to)
+        return remote(src, dst, y_s.at[n // 3], y_r.at[n], to)
 
     def e1_blk(xx, kk, half_, n):
         rows = pl.multiple_of((xx * 2 + kk) * BW + half_ * VAL, VAL)
@@ -212,15 +212,15 @@
         ref = e1_blk(xx, kk, 0, BW)
         return remote(ref, ref, e_s, e_r.at[2], sib)
 
-    lo_rows, hi_rows = pl.ds(0, 128), pl.ds(128, 128)
+    pieces = ((0, 64), (64, 96), (160, 96))
     dy_cp = [
-        yh_cp(0, dy_h.at[lo_rows, other_cols], lhs.at[pl.ds(288, 128), zcol], cross),
-        yh_cp(1, dy_h.at[hi_rows, other_cols], lhs.at[pl.ds(416, 128), zcol], cross),
-        yh_cp(1, vdy_h.at[:, other_cols], lhs.at[pl.ds(544, VAL), zcol], cross),
+        yh_cp(n, dy_h.at[pl.ds(a, r), other_cols], lhs.at[pl.ds(288 + a, r), zcol], cross)
+        for n, (a, r) in enumerate(pieces)
     ]
+    dy_cp.append(yh_cp(2, vdy_h.at[:, other_cols], lhs.at[pl.ds(544, VAL), zcol], cross))
     v_cp = [
-        yh_cp(2, vv.at[own_rows, pl.ds(0, VA)], vv.at[own_rows, pl.ds(0, VA)], ypart),
-        yh_cp(2, vv.at[own_rows, pl.ds(VA, VB)], vv.at[own_rows, pl.ds(VA, VB)], ypart),
+        yh_cp(3, vv.at[own_rows, pl.ds(0, VA)], vv.at[own_rows, pl.ds(0, VA)], ypart),
+        yh_cp(3, vv.at[own_rows, pl.ds(VA, VB)], vv.at[own_rows, pl.ds(VA, VB)], ypart),
     ]
     for cp in dy_cp + e1_cp:
         cp.start()
@@ -229,7 +229,8 @@
 
     def z_dy(n, d, zz):
         ref = lhs.at[
-            pl.ds(288 + n * 128, 128 + n * 32), pl.ds(pl.multiple_of(zz * 512, 512), 512)
+            pl.ds(288 + (0, 64, 160)[n], (64, 96, 128)[n]),
+            pl.ds(pl.multiple_of(zz * 512, 512), 512),
         ]
         return remote(ref, ref, z_s.at[0], z_r.at[0], zdev[d - 1])
 
@@ -239,16 +240,15 @@
             iop.at[pl.ds(to * 2, 2)], ior.at[d - 1], z_s.at[1], z_r.at[1], zdev[d - 1]
         )
 
-    def z_ag(d, zz):
-        ref = iof.at[pl.ds(zz * 2, 2)]
+    def z_ag(d):
+        ref = iof.at[z * 2 + yl]
         return remote(ref, ref, z_s.at[2], z_r.at[2], zdev[d - 1])
 
-    def yl_rs():
+    def yl_half():
         return remote(iosb, ioy, z_s.at[3], z_r.at[3], ylp)
 
-    def yl_ag(who):
-        ref = iof.at[z * 2 + who]
-        return remote(ref, ref, z_s.at[4], z_r.at[4], ylp)
+    def yl_all():
+        return remote(iofb, iofo, z_s.at[4], z_r.at[4], ylp)
 
     def part_cp(s):
         return remote(psend.at[s], precv.at[s], p_s, p_r.at[s], ypart)
@@ -291,10 +291,11 @@
 
     cacc[...] = jnp.zeros_like(cacc)
     hacc[...] = jnp.zeros_like(hacc)
-    with scope("dyA"):
-        dy_cp[0].wait_recv()
-        for d in (1, 2, 3):
-            z_dy(0, d, z).start()
+    for n in (0, 1):
+        with scope("dyA"):
+            dy_cp[n].wait_recv()
+            for d in (1, 2, 3):
+                z_dy(n, d, z).start()
 
     def step(i, carry):
         @pl.when(i < NC)
@@ -309,9 +310,9 @@
         @pl.when(i == 0)
         def _():
             with scope("dyB"):
-                take(lhs.at[pl.ds(0, 160), pl.ds(0, 512)], y_r.at[1])
+                take(lhs.at[pl.ds(0, 128), pl.ds(0, 512)], y_r.at[2])
                 for d in (1, 2, 3):
-                    z_dy(1, d, z).start()
+                    z_dy(2, d, z).start()
             with scope("e1x"):
                 local_wait(1)
                 take(e1.at[pl.ds(0, 3 * VAL), :], e_r.at[0])
@@ -350,7 +351,7 @@
         @pl.when(i == NC - 1)
         def _():
             with scope("vown"):
-                take(vv.at[pl.ds(0, VAL), :], y_r.at[2])
+                take(vv.at[pl.ds(0, VAL), :], y_r.at[3])
                 varing.own()
                 vbring.own()
 
@@ -368,6 +369,11 @@
 
         @pl.when(i == 10)
         def _():
+            with scope("ylhalf"):
+                yl_half().wait_recv()
+                iof[z * 2 + yl] = ios[yl] + ioy[...].astype(F32)
+                for d in (1, 2, 3):
+                    z_ag(d).start()
             with scope("vgfwd"):
                 varing.forward()
 
@@ -377,7 +383,7 @@
                 take(ior, z_r.at[1])
                 ios[...] = iop[pl.ds(z * 2, 2)] + ior[0] + ior[1] + ior[2]
                 iosb[...] = ios[1 - yl].astype(BF)
-                yl_rs().start()
+                yl_half().start()
 
         @pl.when(i == 5)
         def _():
@@ -398,54 +404,53 @@
             with scope("vcfwd"):
                 vcring(i - 10).forward()
 
-        @pl.when(i == 11)
-        def _():
-            with scope("ylrs"):
-                yl_rs().wait_recv()
-                iof[z * 2 + yl] = (ios[yl] + ioy[...].astype(F32)).astype(BF)
-                yl_ag(yl).start()
-
         @pl.when(i == NC + 6)
         def _():
-            with scope("ylag"):
-                yl_ag(1 - yl).wait_recv()
-                for d in (1, 2, 3):
-                    z_ag(d, z).start()
+            with scope("zag"):
+                take(iof.at[pl.ds(0, 3)], z_r.at[2])
+                for q in range(4):
+                    iofb[q] = iof[q * 2 + yl].astype(BF)
+                yl_all().start()
 
         return carry
 
     lax.fori_loop(0, NC + 7, step, 0)
     with scope("tailA"):
         vcring(4).forward()
+        vcring(5).forward()
         varing.last()
         for m in range(4):
             vcring(m).last()
         varing.full()
     for m in range(NC):
-        with scope("tail"):
+        with scope("tail%d" % m):
             if m == 1:
-                vcring(5).forward()
-            if m == 2:
+                vcring(6).forward()
                 vbring.last()
-                vcring(6).forward()
             if m == 3:
                 vcring(4).last()
+                vcring(5).last()
             if m == 4:
                 vbring.full()
-                vcring(5).last()
             if m == 5:
                 vcring(6).last()
         with scope("gram"):
             gram_stage(m)
 
-    with scope("zag"):
-        take(iof.at[pl.ds(0, 6)], z_r.at[2])
+    with scope("ylall"):
+        yl_all().wait_recv()
     for v in (0, 1):
         acc = jnp.zeros((VAL, TOK), F32)
-        for p in range(8):
-            r = slice(p * 64 + v * VAL, p * 64 + v * VAL + VAL)
-            q = slice(v * VAL, v * VAL + VAL)
-            acc += iof[p, 0, q, :].astype(F32) * cacc[r, :] + iof[p, 1, q, :].astype(F32) * hacc[r, :]
+        at = slice(v * VAL, v * VAL + VAL)
+        for q in range(4):
+            for who in (0, 1):
+                side = yl if who == 0 else 1 - yl
+                r = pl.ds(pl.multiple_of((q * 2 + side) * BW + v * VAL, VAL), VAL)
+                if who == 0:
+                    gi, go = iof[q * 2 + yl, 0, at, :], iof[q * 2 + yl, 1, at, :]
+                else:
+                    gi, go = iofo[q, 0, at, :].astype(F32), iofo[q, 1, at, :].astype(F32)
+                acc += gi * cacc[r, :] + go * hacc[r, :]
         acc = acc[:, 0:128] + acc[:, 128:256]
         acc = acc[0:8] + acc[8:16] + acc[16:24] + acc[24:32]
         fin_s[v * 4 : v * 4 + 4, :] = acc[0:4] + acc[4:8]
@@ -460,9 +465,9 @@
     take(psend, p_s)
     take(lhs.at[pl.ds(0, 288), pl.ds(0, 1536)], z_s.at[0])
     take(ior, z_s.at[1])
-    take(iof.at[pl.ds(0, 6)], z_s.at[2])
+    take(iof.at[pl.ds(0, 3)], z_s.at[2])
     take(iosb, z_s.at[3])
-    take(ioy, z_s.at[4])
+    take(iofb, z_s.at[4])
     with scope("finwait"):
         take(fin_r, f_r)
         take(fin_r, f_s)
@@ -519,7 +524,9 @@
             vm((2, 2, 64, TOK), F32),
             vm((2, 64, TOK), BF),
             vm((2, 64, TOK), BF),
-            vm((8, 2, 64, TOK), BF),
+            vm((8, 2, 64, TOK), F32),
+            vm((4, 2, 64, TOK), BF),
+            vm((4, 2, 64, TOK), BF),
             vm((512, TOK), F32),
             vm((512, TOK), F32),
             vm((8, 128), F32),
@@ -530,7 +537,7 @@
             dma,
             dma((3,)),
             dma((2,)),
-            dma((3,)),
+            dma((4,)),
             dma,
             dma((NC,)),
             dma((5,)),

time: 75.6 us -> 75 us (level)
  no operation moved by 1% of the time
where the time goes in v4:
time: 75 us; the launch traced here: 74.9 us
  Pallas kernels  74.2 us (99%)
    pallas_call x1, Pallas kernels, per_device(): pl.pallas_call(kernel, out_shape=(vm((TOK, FFL), BF), vm((TOK, FFL), BF),...  72.4 us
    pallas_call x1, Pallas kernels, per_device(): pl.pallas_call(publish, out_shape=(jax.ShapeDtypeStruct((TOK, FFL), BF),...  1.8 us

profile of v4, /device:TPU:1, one launch (start us, length us, event | category | flops | bytes accessed | tf_op | source)
XLA Modules:
  0.0 74.9 jit_solution(11215689815815070305)
XLA Ops:
  0.6 72.4 %shard_map.112 = (bf16[256,1792]{1,0:T(8,128)(2,1)S(1)}, bf16[256,1792]{1,0:T(8,128)(2,1)S(1)}, f32[8,128]{1,0:T(8,128)S(1)}) custom-call(bf16[256,512]{1,0:T(8,128)(2,1)} %tx_h.1, bf16[256,1792]{1,0:T(8,128)(2,1)} %gate_h.1, bf16[256,1792]{1,0:T(8,128)(2,1)} %up_h.1, bf16[256,4096]{1,0:T(8,128)(2,1)} %dy_h.1, bf16[32,512]{1,0:T(8,128)(2,1)} %vx_h.1, ...), custom_call_target="tpu_custom_call" | custom-call | tf_op jit(solution)/shard_map/pallas_call | solution.py:503
  73.1 1.8 %shard_map.113 = (bf16[256,1792]{1,0:T(8,128)(2,1)}, bf16[256,1792]{1,0:T(8,128)(2,1)}, f32[1,2]{1,0:T(1,128)}) custom-call(bf16[256,1792]{1,0:T(8,128)(2,1)S(1)} %get-tuple-element.6.gg, bf16[256,1792]{1,0:T(8,128)(2,1)S(1)} %get-tuple-element.7.ug, f32[8,128]{1,0:T(8,128)S(1)} %get-tuple-element.8.total), custom_call_target="tpu_custom_call" | custom-call | tf_op jit(solution)/shard_map/pallas_call | solution.py:553

commit v5 on v4

--- a/solution.py
+++ b/solution.py
@@ -222,9 +222,12 @@
         yh_cp(3, vv.at[own_rows, pl.ds(0, VA)], vv.at[own_rows, pl.ds(0, VA)], ypart),
         yh_cp(3, vv.at[own_rows, pl.ds(VA, VB)], vv.at[own_rows, pl.ds(VA, VB)], ypart),
     ]
-    for cp in dy_cp + e1_cp:
+    for cp in dy_cp:
         cp.start()
-    for c in range(LEAD):
+    wown(0)
+    for cp in e1_cp:
+        cp.start()
+    for c in range(1, LEAD):
         wown(c)
 
     def z_dy(n, d, zz):

time: 75 us -> 75 us (level)
  no operation moved by 1% of the time
where the time goes in v5:
time: 75 us; the launch traced here: 74.9 us
  Pallas kernels  74.3 us (99%)
    pallas_call x1, Pallas kernels, per_device(): pl.pallas_call(kernel, out_shape=(vm((TOK, FFL), BF), vm((TOK, FFL), BF),...  72.5 us
    pallas_call x1, Pallas kernels, per_device(): pl.pallas_call(publish, out_shape=(jax.ShapeDtypeStruct((TOK, FFL), BF),...  1.8 us

profile of v5, /device:TPU:1, one launch (start us, length us, event | category | flops | bytes accessed | tf_op | source)
XLA Modules:
  0.0 74.9 jit_solution(1496803040693453454)
XLA Ops:
  0.6 72.5 %shard_map.112 = (bf16[256,1792]{1,0:T(8,128)(2,1)S(1)}, bf16[256,1792]{1,0:T(8,128)(2,1)S(1)}, f32[8,128]{1,0:T(8,128)S(1)}) custom-call(bf16[256,512]{1,0:T(8,128)(2,1)} %tx_h.1, bf16[256,1792]{1,0:T(8,128)(2,1)} %gate_h.1, bf16[256,1792]{1,0:T(8,128)(2,1)} %up_h.1, bf16[256,4096]{1,0:T(8,128)(2,1)} %dy_h.1, bf16[32,512]{1,0:T(8,128)(2,1)} %vx_h.1, ...), custom_call_target="tpu_custom_call" | custom-call | tf_op jit(solution)/shard_map/pallas_call | solution.py:506
  73.1 1.8 %shard_map.113 = (bf16[256,1792]{1,0:T(8,128)(2,1)}, bf16[256,1792]{1,0:T(8,128)(2,1)}, f32[1,2]{1,0:T(1,128)}) custom-call(bf16[256,1792]{1,0:T(8,128)(2,1)S(1)} %get-tuple-element.6.gg, bf16[256,1792]{1,0:T(8,128)(2,1)S(1)} %get-tuple-element.7.ug, f32[8,128]{1,0:T(8,128)S(1)} %get-tuple-element.8.total), custom_call_target="tpu_custom_call" | custom-call | tf_op jit(solution)/shard_map/pallas_call | solution.py:556
